TPU v7x, 512 devices: a whole 4x4x16 slice. The times are simulated.
512 devices in a mesh: elem: 32 (over x_lo, z), band: 16 (over x_hi, y, core).
Axes of the slice: x: 4 (x_hi: 2, x_lo: 2; x = x_hi * 2 + x_lo), y: 4, z: 16, core: 2. Of those that a mesh axis runs over, the one named last changes fastest.
Arguments:
- basis_sizes: int32 [512], P('elem'), may hold values from 96 to 160, as said below
- coupling_pattern: int32 [512], P('elem'), may hold values 0 or 1
- h_diag: bfloat16 [512, 160, 160], P('elem'), may hold values from -0.6708204 to 0.6708204, as said below
- h_couple: bfloat16 [512, 160, 160], P('elem'), may hold values from -0.25 to 0.25
- bands: bfloat16 [1024, 81920], P('band', 'elem'), may hold values from -1500 to 1500
Outputs:
- filtered: bfloat16 [1024, 81920], P('band', 'elem')
Inputs may be any that keep to these rules, and one draw needn't show every extreme that they name: `basis_sizes`: every element has between 96 and 160 basis functions; some element has exactly 160 and some exactly 96. `h_diag`: each block is symmetric.
All inputs are finite; a program needn't handle non-finite values. No bound on the sum of `coupling_pattern` on one device may be relied on, other than what follows from the above.
Results may differ from a plain program's by a relative error of at most 0.0085.
Values may be sent and summed in bfloat16 or wider, within the bound.
A program may use at most 64 MiB of HBM per device.

v0:
```python
import math

import jax
import jax.numpy as jnp
from jax import lax
from jax.sharding import PartitionSpec as P

DEGREE = 6


center_shift = 0.4
half_width = 2.8
epsilon_norm = 1e-06


def from_behind(value, axis, steps):
    count = lax.axis_size(axis)
    pairs = [(source, (source + steps) % count) for source in range(count)]
    return lax.ppermute(value, axis, pairs)


def with_halo(array, sides, width):
    for axis, dim in sides:
        count, length = (lax.axis_size(axis), array.shape[dim])
        up = [(i, (i + 1) % count) for i in range(count)]
        down = [(j, i) for i, j in up]
        last = lax.slice_in_dim(array, length - width, length, axis=dim)
        leading = lax.slice_in_dim(array, 0, width, axis=dim)
        before = lax.ppermute(last, axis, up)
        after = lax.ppermute(leading, axis, down)
        array = jnp.concatenate([before, array, after], axis=dim)
    return array


def cut_along(array, dim, count):
    before, after = (array.shape[:dim], array.shape[dim + 1 :])
    return jnp.moveaxis(array.reshape(*before, count, -1, *after), dim, 0)


def sent_and_summed(array, axis, dim):
    pieces = cut_along(array, dim, lax.axis_size(axis))
    arrived = lax.all_to_all(pieces, axis, split_axis=0, concat_axis=0, tiled=True)
    return arrived.sum(axis=0)


def padded_to(lines, count):
    spare = -len(lines) % count
    return jnp.pad(lines, [(0, spare)] + [(0, 0)] * (lines.ndim - 1))


def in_order(pieces, dim):
    pieces = jnp.moveaxis(pieces, 0, dim)
    dims = pieces.shape
    return pieces.reshape(*dims[:dim], dims[dim] * dims[dim + 1], *dims[dim + 2 :])


def from_everyone(array, axis):
    count = lax.axis_size(axis)
    return lax.all_to_all(
        jnp.broadcast_to(array[None], (count, *array.shape)), axis, 0, 0, tiled=True
    )


def gathered_copies(array, axis, dim):
    return in_order(from_everyone(array, axis), dim)


def nested_sum(array, axes):
    own = sent_and_summed(padded_to(array, lax.axis_size(axes)), axes, 0)
    whole = gathered_copies(own, axes, 0)
    return whole[: len(array)].reshape(array.shape)


def in_one(arrays, axis):
    line, at, done = (jnp.concatenate([a.reshape(-1) for a in arrays]), 0, [])
    running = nested_sum(line, axis)
    for a in arrays:
        done.append(running[at : at + a.size].reshape(a.shape))
        at += a.size
    return tuple(done)


def identity_block(shape, offset):
    row_ids = lax.broadcasted_iota(jnp.int32, shape, 0) + offset
    col_ids = lax.broadcasted_iota(jnp.int32, shape, 1)
    return (row_ids == col_ids).astype(jnp.float32)


def rotation_columns(gram_strip, scales, offset, total_rows):
    own_scales = lax.dynamic_slice_in_dim(scales, offset, gram_strip.shape[0], 0)
    identity = identity_block(gram_strip.shape, offset)
    normed = own_scales[:, None] * gram_strip * scales[None, :]
    return (math.sqrt(total_rows) * scales[None, :] * (1.5 * identity - 0.5 * normed)).astype(
        jnp.bfloat16
    )


def shards(basis_sizes, coupling_pattern, h_diag, h_couple, bands):
    elem_local = h_diag.shape[0]
    basis_width = h_diag.shape[1]
    band_local = bands.shape[0]
    total_rows = elem_local * lax.axis_size("elem") * basis_width
    columns = lax.broadcasted_iota(jnp.int32, (elem_local, basis_width), 1)
    valid_rows = (columns < basis_sizes[:, None]).astype(jnp.float32)
    coupling = h_couple * coupling_pattern.astype(jnp.bfloat16)[:, None, None]
    current = (
        bands.reshape(band_local, elem_local, basis_width) * valid_rows.astype(jnp.bfloat16)[None]
    )
    prior_block = from_behind(coupling[-1], "elem", 1)
    behind = jnp.concatenate([prior_block[None], coupling[:-1]], axis=0)
    previous = current
    for degree in range(DEGREE):
        current_float = current.astype(jnp.float32)
        local_term = jnp.einsum("eij,bej->bei", h_diag, current, preferred_element_type=jnp.float32)
        rimmed = with_halo(current, (("elem", 1),), 1)
        upper_term = jnp.einsum(
            "eij,bej->bei", coupling, rimmed[:, 2:], preferred_element_type=jnp.float32
        )
        lower_term = jnp.einsum(
            "eji,bej->bei", behind, rimmed[:, :-2], preferred_element_type=jnp.float32
        )
        applied = (local_term + upper_term + lower_term) * valid_rows[None]
        shifted = applied - center_shift * current_float
        if degree == 0:
            next_iterate = shifted / half_width
        else:
            next_iterate = 2.0 * shifted / half_width - previous.astype(jnp.float32)
        previous, current = (current, next_iterate.astype(jnp.bfloat16))
    filtered = current.reshape(band_local, elem_local * basis_width)
    every_band = lax.all_gather(filtered, "band", axis=0, tiled=True)
    strip = lax.dot_general(
        filtered, every_band, (((1,), (1,)), ((), ())), preferred_element_type=jnp.float32
    )
    squares = jnp.sum(jnp.square(every_band.astype(jnp.float32)), axis=1)
    strip, squares = in_one((strip, squares), "elem")
    scales = lax.rsqrt(squares + epsilon_norm)
    offset = lax.axis_index("band") * band_local
    weights = rotation_columns(strip, scales, offset, total_rows)
    return jnp.dot(weights, every_band, preferred_element_type=jnp.float32).astype(jnp.bfloat16)


def solution(mesh):
    in_specs = (
        P("elem"),
        P("elem"),
        P("elem", None, None),
        P("elem", None, None),
        P("band", "elem"),
    )
    out_specs = P("band", "elem")
    return jax.shard_map(shards, mesh=mesh, in_specs=in_specs, out_specs=out_specs, check_vma=False)
```

profile of v0, /device:TPU:1, one launch (start us, length us, event | category | flops | bytes accessed | tf_op | source)
XLA Modules:
  0.0 233.2 jit_solution(5489966992753871043)
XLA Ops:
  6.5 0.9 fusion.79
  7.4 1.6 reshape.59
  9.2 4.4 %collective-permute-start.1 = (bf16[64,1,160]{2,0,1:T(8,128)(2,1)S(1)}, bf16[64,1,160]{2,0,1:T(8,128)(2,1)S(1)}, u32[]{:S(2)}, u32[]{:S(2)}) collective-permute-start(bf16[64,1,160]{2,0,1:T(8,128)(2,1)S(1)} %get-tuple-element.15), channel_id=1, source_target_pairs={{0,16},{16,32},{32,48},{48,64},{64,80},{80,96},{96,112},{112,128},... | collective-permute-start | bytes 61448 | tf_op jit(solution)/shard_map/ppermute | solution.py:29
  13.6 10.4 %collective-permute-start = (bf16[64,1,160]{2,0,1:T(8,128)(2,1)S(1)}, bf16[64,1,160]{2,0,1:T(8,128)(2,1)S(1)}, u32[]{:S(2)}, u32[]{:S(2)}) collective-permute-start(bf16[64,1,160]{2,0,1:T(8,128)(2,1)S(1)} %get-tuple-element.16), channel_id=1, source_target_pairs={{16,0},{32,16},{48,32},{64,48},{80,64},{96,80},{112,96},{128,112},... | collective-permute-start | bytes 61448 | tf_op jit(solution)/shard_map/ppermute | solution.py:30
  24.2 1.9 collective-permute-start.2
  26.2 0.6 fusion.103
  26.8 0.5 convolution_add_fusion.11
  27.4 4.2 %collective-permute-done.2 = bf16[160,160]{1,0:T(8,128)(2,1)S(1)} collective-permute-done((bf16[160,160]{1,0:T(8,128)(2,1)S(1)}, bf16[160,160]{1,0:T(8,128)(2,1)S(1)}, u32[]{:S(2)}, u32[]{:S(2)}) %collective-permute-start.2) | collective-permute-done | bytes 51232 | tf_op jit(solution)/shard_map/ppermute | solution.py:19
  32.0 1.9 collective-permute-start.3
  33.9 0.6 fusion.104
  34.5 3.4 %collective-permute-start.4 = (bf16[64,1,160]{2,0,1:T(8,128)(2,1)S(1)}, bf16[64,1,160]{2,0,1:T(8,128)(2,1)S(1)}, u32[]{:S(2)}, u32[]{:S(2)}) collective-permute-start(bf16[64,1,160]{2,0,1:T(8,128)(2,1)S(1)} %get-tuple-element.13), channel_id=1, source_target_pairs={{0,16},{16,32},{32,48},{48,64},{64,80},{80,96},{96,112},{112,128},... | collective-permute-start | bytes 61448 | tf_op jit(solution)/shard_map/ppermute | solution.py:29
  37.8 0.5 convolution_add_fusion.9
  38.4 2.8 %collective-permute-done.4 = bf16[64,1,160]{2,0,1:T(8,128)(2,1)S(1)} collective-permute-done((bf16[64,1,160]{2,0,1:T(8,128)(2,1)S(1)}, bf16[64,1,160]{2,0,1:T(8,128)(2,1)S(1)}, u32[]{:S(2)}, u32[]{:S(2)}) %collective-permute-start.4) | collective-permute-done | bytes 20512 | tf_op jit(solution)/shard_map/ppermute | solution.py:29
  41.2 0.5 fusion.25
  41.8 1.9 collective-permute-start.5
  43.7 0.6 fusion.105
  44.2 3.4 %collective-permute-start.6 = (bf16[64,1,160]{2,0,1:T(8,128)(2,1)S(1)}, bf16[64,1,160]{2,0,1:T(8,128)(2,1)S(1)}, u32[]{:S(2)}, u32[]{:S(2)}) collective-permute-start(bf16[64,1,160]{2,0,1:T(8,128)(2,1)S(1)} %get-tuple-element.11), channel_id=1, source_target_pairs={{0,16},{16,32},{32,48},{48,64},{64,80},{80,96},{96,112},{112,128},... | collective-permute-start | bytes 61448 | tf_op jit(solution)/shard_map/ppermute | solution.py:29
  47.6 0.5 convolution_add_fusion.7
  48.2 2.8 %collective-permute-done.6 = bf16[64,1,160]{2,0,1:T(8,128)(2,1)S(1)} collective-permute-done((bf16[64,1,160]{2,0,1:T(8,128)(2,1)S(1)}, bf16[64,1,160]{2,0,1:T(8,128)(2,1)S(1)}, u32[]{:S(2)}, u32[]{:S(2)}) %collective-permute-start.6) | collective-permute-done | bytes 20512 | tf_op jit(solution)/shard_map/ppermute | solution.py:29
  51.0 0.5 fusion.26
  51.6 1.9 collective-permute-start.7
  53.5 0.6 fusion.106
  54.0 3.4 %collective-permute-start.8 = (bf16[64,1,160]{2,0,1:T(8,128)(2,1)S(1)}, bf16[64,1,160]{2,0,1:T(8,128)(2,1)S(1)}, u32[]{:S(2)}, u32[]{:S(2)}) collective-permute-start(bf16[64,1,160]{2,0,1:T(8,128)(2,1)S(1)} %get-tuple-element.9), channel_id=1, source_target_pairs={{0,16},{16,32},{32,48},{48,64},{64,80},{80,96},{96,112},{112,128},... | collective-permute-start | bytes 61448 | tf_op jit(solution)/shard_map/ppermute | solution.py:29
  57.4 0.5 convolution_add_fusion.5
  58.0 2.8 %collective-permute-done.8 = bf16[64,1,160]{2,0,1:T(8,128)(2,1)S(1)} collective-permute-done((bf16[64,1,160]{2,0,1:T(8,128)(2,1)S(1)}, bf16[64,1,160]{2,0,1:T(8,128)(2,1)S(1)}, u32[]{:S(2)}, u32[]{:S(2)}) %collective-permute-start.8) | collective-permute-done | bytes 20512 | tf_op jit(solution)/shard_map/ppermute | solution.py:29
  60.8 0.5 fusion.27
  61.3 1.9 collective-permute-start.9
  63.3 0.6 fusion.107
  63.8 3.4 %collective-permute-start.10 = (bf16[64,1,160]{2,0,1:T(8,128)(2,1)S(1)}, bf16[64,1,160]{2,0,1:T(8,128)(2,1)S(1)}, u32[]{:S(2)}, u32[]{:S(2)}) collective-permute-start(bf16[64,1,160]{2,0,1:T(8,128)(2,1)S(1)} %get-tuple-element.7), channel_id=1, source_target_pairs={{0,16},{16,32},{32,48},{48,64},{64,80},{80,96},{96,112},{112,128},... | collective-permute-start | bytes 61448 | tf_op jit(solution)/shard_map/ppermute | solution.py:29
  67.2 0.5 convolution_add_fusion.3
  67.8 2.8 %collective-permute-done.10 = bf16[64,1,160]{2,0,1:T(8,128)(2,1)S(1)} collective-permute-done((bf16[64,1,160]{2,0,1:T(8,128)(2,1)S(1)}, bf16[64,1,160]{2,0,1:T(8,128)(2,1)S(1)}, u32[]{:S(2)}, u32[]{:S(2)}) %collective-permute-start.10) | collective-permute-done | bytes 20512 | tf_op jit(solution)/shard_map/ppermute | solution.py:29
  70.6 0.5 fusion.28
  71.1 1.9 collective-permute-start.11
  73.1 0.6 fusion.108
  73.6 3.5 %collective-permute-start.12 = (bf16[64,1,160]{2,0,1:T(8,128)(2,1)S(1)}, bf16[64,1,160]{2,0,1:T(8,128)(2,1)S(1)}, u32[]{:S(2)}, u32[]{:S(2)}) collective-permute-start(bf16[64,1,160]{2,0,1:T(8,128)(2,1)S(1)} %get-tuple-element.5), channel_id=1, source_target_pairs={{0,16},{16,32},{32,48},{48,64},{64,80},{80,96},{96,112},{112,128},... | collective-permute-start | bytes 61448 | tf_op jit(solution)/shard_map/ppermute | solution.py:29
  77.2 0.5 convolution_add_fusion.1
  77.7 2.7 %collective-permute-done.12 = bf16[64,1,160]{2,0,1:T(8,128)(2,1)S(1)} collective-permute-done((bf16[64,1,160]{2,0,1:T(8,128)(2,1)S(1)}, bf16[64,1,160]{2,0,1:T(8,128)(2,1)S(1)}, u32[]{:S(2)}, u32[]{:S(2)}) %collective-permute-start.12) | collective-permute-done | bytes 20512 | tf_op jit(solution)/shard_map/ppermute | solution.py:29
  80.4 0.5 fusion.29
  81.2 1.5 reshape.60
  82.7 74.1 %all-gather.2.cloned.1.call-done = bf16[1024,2560]{1,0:T(8,128)(2,1)} async-done(((bf16[64,2560]{1,0:T(8,128)(2,1)}), bf16[1024,2560]{1,0:T(8,128)(2,1)}) %all-gather.2.cloned.1.call-update) | async-done | bytes 5242896 | tf_op jit(solution)/shard_map/all_gather | solution.py:130
  156.8 4.4 %convolution_bitcast_fusion = f32[8,8,8,128]{3,2,1,0:T(8,128)S(1)} fusion(bf16[64,2560]{1,0:T(8,128)(2,1)} %reshape.60, bf16[1024,2560]{1,0:T(8,128)(2,1)} %all-gather.2.cloned.1.call-done), kind=kOutput, calls=%fused_computation.55 | convolution fusion | flops 335544320 | bytes 5832704 | tf_op jit(solution)/shard_map/dot_general | solution.py:131
  161.3 1.1 multiply_reduce_fusion
  162.8 33.2 %all_to_all.15 = f32[32,1,2080]{2,1,0:T(1,128)S(1)} all-to-all(f32[32,1,2080]{2,1,0:T(1,128)S(1)} %all_to_all.10), channel_id=1, replica_groups=mesh['elem'=32,'band'=16] {'elem'}, dimensions={0} | all-to-all | bytes 532480 | tf_op jit(solution)/shard_map/all_to_all | solution.py:42
  196.1 0.9 broadcast_in_dim.5
  197.0 4.7 %all-to-all-start.1 = ((f32[32,1,2080]{2,1,0:T(1,128)}), f32[32,1,2080]{2,1,0:T(1,128)S(1)}, u32[]{:S(2)}, u32[]{:S(2)}) async-start(f32[32,1,2080]{2,1,0:T(1,128)} %broadcast_in_dim.5), calls=%async_computation.1 | async-start | bytes 557056 | tf_op jit(solution)/shard_map/all_to_all | solution.py:59
  201.7 19.2 %all-to-all-done.1 = f32[32,1,2080]{2,1,0:T(1,128)S(1)} async-done(((f32[32,1,2080]{2,1,0:T(1,128)}), f32[32,1,2080]{2,1,0:T(1,128)S(1)}, u32[]{:S(2)}, u32[]{:S(2)}) %all-to-all-start.1) | async-done | bytes 266272 | tf_op jit(solution)/shard_map/all_to_all | solution.py:59
  220.8 0.7 reduce.1
  222.1 4.3 %convolution_convert_fusion = bf16[64,2560]{1,0:T(8,128)(2,1)} fusion(bf16[1024,2560]{1,0:T(8,128)(2,1)} %all-gather.2.cloned.1.call-done, f32[65,1024]{1,0:T(8,128)S(1)} %slice.126, f32[1024]{0:T(1024)S(1)} %get-tuple-element.18, f32[64]{0:T(128)S(1)} %dynamic_slice.3, s32[64]{0:T(128)S(1)} %iota_add_fusion, f32[1024]{0:T(1024)S(1)} %get-tuple-element.17), kind=kOutput, calls=%fused_computation.1 | convolution fusion | flops 336232448 | bytes 5841920 | tf_op jit(solution)/shard_map/dot_general | solution.py:139
  (39 shorter events, 2.4 us)
Async XLA Ops:
  6.5 19.6 %copy-start = (bf16[16,160,160]{2,1,0:T(8,128)(2,1)S(1)}, bf16[16,160,160]{2,1,0:T(8,128)(2,1)}, u32[]{:S(2)}) copy-start(bf16[16,160,160]{2,1,0:T(8,128)(2,1)} %param.7) | copy-start | bytes 2457604
  6.5 17.5 %copy-start.3 = (s32[16]{0:T(128)S(1)}, s32[16]{0:T(128)}, u32[]{:S(2)}) copy-start(s32[16]{0:T(128)} %param.6) | copy-start | bytes 196
  6.5 17.5 %copy-start.2 = (bf16[16,160,160]{2,1,0:T(8,128)(2,1)S(1)}, bf16[16,160,160]{2,1,0:T(8,128)(2,1)}, u32[]{:S(2)}) copy-start(bf16[16,160,160]{2,1,0:T(8,128)(2,1)} %param.8) | copy-start | bytes 2457604
  6.5 150.2 %all-gather.2.cloned.1.call-start = ((), (), s32[]{:S(2)}) async-start(), calls=%async_computation.2 | async-start | bytes 5570560 | tf_op jit(solution)/shard_map/all_gather | solution.py:130
  9.2 18.2 %collective-permute-start.1 = (bf16[64,1,160]{2,0,1:T(8,128)(2,1)S(1)}, bf16[64,1,160]{2,0,1:T(8,128)(2,1)S(1)}, u32[]{:S(2)}, u32[]{:S(2)}) collective-permute-start(bf16[64,1,160]{2,0,1:T(8,128)(2,1)S(1)} %get-tuple-element.15), channel_id=1, source_target_pairs={{0,16},{16,32},{32,48},{48,64},{64,80},{80,96},{96,112},{112,128},... | collective-permute-start | bytes 61448 | tf_op jit(solution)/shard_map/ppermute | solution.py:29
  13.6 13.2 %collective-permute-start = (bf16[64,1,160]{2,0,1:T(8,128)(2,1)S(1)}, bf16[64,1,160]{2,0,1:T(8,128)(2,1)S(1)}, u32[]{:S(2)}, u32[]{:S(2)}) collective-permute-start(bf16[64,1,160]{2,0,1:T(8,128)(2,1)S(1)} %get-tuple-element.16), channel_id=1, source_target_pairs={{16,0},{32,16},{48,32},{64,48},{80,64},{96,80},{112,96},{128,112},... | collective-permute-start | bytes 61448 | tf_op jit(solution)/shard_map/ppermute | solution.py:30
  24.2 7.3 %collective-permute-start.2 = (bf16[160,160]{1,0:T(8,128)(2,1)S(1)}, bf16[160,160]{1,0:T(8,128)(2,1)S(1)}, u32[]{:S(2)}, u32[]{:S(2)}) collective-permute-start(bf16[160,160]{1,0:T(8,128)(2,1)S(1)} %slice_bitcast_fusion), channel_id=1, source_target_pairs={{0,16},{16,32},{32,48},{48,64},{64,80},{80,96},{96,112},{112,128},... | collective-permute-start | bytes 153608 | tf_op jit(solution)/shard_map/ppermute | solution.py:19
  32.0 5.9 %collective-permute-start.3 = (bf16[64,1,160]{2,0,1:T(8,128)(2,1)S(1)}, bf16[64,1,160]{2,0,1:T(8,128)(2,1)S(1)}, u32[]{:S(2)}, u32[]{:S(2)}) collective-permute-start(bf16[64,1,160]{2,0,1:T(8,128)(2,1)S(1)} %get-tuple-element.14), channel_id=1, source_target_pairs={{16,0},{32,16},{48,32},{64,48},{80,64},{96,80},{112,96},{128,112},... | collective-permute-start | bytes 61448 | tf_op jit(solution)/shard_map/ppermute | solution.py:30
  34.5 6.8 %collective-permute-start.4 = (bf16[64,1,160]{2,0,1:T(8,128)(2,1)S(1)}, bf16[64,1,160]{2,0,1:T(8,128)(2,1)S(1)}, u32[]{:S(2)}, u32[]{:S(2)}) collective-permute-start(bf16[64,1,160]{2,0,1:T(8,128)(2,1)S(1)} %get-tuple-element.13), channel_id=1, source_target_pairs={{0,16},{16,32},{32,48},{48,64},{64,80},{80,96},{96,112},{112,128},... | collective-permute-start | bytes 61448 | tf_op jit(solution)/shard_map/ppermute | solution.py:29
  41.8 5.9 %collective-permute-start.5 = (bf16[64,1,160]{2,0,1:T(8,128)(2,1)S(1)}, bf16[64,1,160]{2,0,1:T(8,128)(2,1)S(1)}, u32[]{:S(2)}, u32[]{:S(2)}) collective-permute-start(bf16[64,1,160]{2,0,1:T(8,128)(2,1)S(1)} %get-tuple-element.12), channel_id=1, source_target_pairs={{16,0},{32,16},{48,32},{64,48},{80,64},{96,80},{112,96},{128,112},... | collective-permute-start | bytes 61448 | tf_op jit(solution)/shard_map/ppermute | solution.py:30
  44.2 6.8 %collective-permute-start.6 = (bf16[64,1,160]{2,0,1:T(8,128)(2,1)S(1)}, bf16[64,1,160]{2,0,1:T(8,128)(2,1)S(1)}, u32[]{:S(2)}, u32[]{:S(2)}) collective-permute-start(bf16[64,1,160]{2,0,1:T(8,128)(2,1)S(1)} %get-tuple-element.11), channel_id=1, source_target_pairs={{0,16},{16,32},{32,48},{48,64},{64,80},{80,96},{96,112},{112,128},... | collective-permute-start | bytes 61448 | tf_op jit(solution)/shard_map/ppermute | solution.py:29
  51.6 5.9 %collective-permute-start.7 = (bf16[64,1,160]{2,0,1:T(8,128)(2,1)S(1)}, bf16[64,1,160]{2,0,1:T(8,128)(2,1)S(1)}, u32[]{:S(2)}, u32[]{:S(2)}) collective-permute-start(bf16[64,1,160]{2,0,1:T(8,128)(2,1)S(1)} %get-tuple-element.10), channel_id=1, source_target_pairs={{16,0},{32,16},{48,32},{64,48},{80,64},{96,80},{112,96},{128,112},... | collective-permute-start | bytes 61448 | tf_op jit(solution)/shard_map/ppermute | solution.py:30
  54.0 6.8 %collective-permute-start.8 = (bf16[64,1,160]{2,0,1:T(8,128)(2,1)S(1)}, bf16[64,1,160]{2,0,1:T(8,128)(2,1)S(1)}, u32[]{:S(2)}, u32[]{:S(2)}) collective-permute-start(bf16[64,1,160]{2,0,1:T(8,128)(2,1)S(1)} %get-tuple-element.9), channel_id=1, source_target_pairs={{0,16},{16,32},{32,48},{48,64},{64,80},{80,96},{96,112},{112,128},... | collective-permute-start | bytes 61448 | tf_op jit(solution)/shard_map/ppermute | solution.py:29
  61.3 5.9 %collective-permute-start.9 = (bf16[64,1,160]{2,0,1:T(8,128)(2,1)S(1)}, bf16[64,1,160]{2,0,1:T(8,128)(2,1)S(1)}, u32[]{:S(2)}, u32[]{:S(2)}) collective-permute-start(bf16[64,1,160]{2,0,1:T(8,128)(2,1)S(1)} %get-tuple-element.8), channel_id=1, source_target_pairs={{16,0},{32,16},{48,32},{64,48},{80,64},{96,80},{112,96},{128,112},... | collective-permute-start | bytes 61448 | tf_op jit(solution)/shard_map/ppermute | solution.py:30
  63.8 6.8 %collective-permute-start.10 = (bf16[64,1,160]{2,0,1:T(8,128)(2,1)S(1)}, bf16[64,1,160]{2,0,1:T(8,128)(2,1)S(1)}, u32[]{:S(2)}, u32[]{:S(2)}) collective-permute-start(bf16[64,1,160]{2,0,1:T(8,128)(2,1)S(1)} %get-tuple-element.7), channel_id=1, source_target_pairs={{0,16},{16,32},{32,48},{48,64},{64,80},{80,96},{96,112},{112,128},... | collective-permute-start | bytes 61448 | tf_op jit(solution)/shard_map/ppermute | solution.py:29
  71.1 6.0 %collective-permute-start.11 = (bf16[64,1,160]{2,0,1:T(8,128)(2,1)S(1)}, bf16[64,1,160]{2,0,1:T(8,128)(2,1)S(1)}, u32[]{:S(2)}, u32[]{:S(2)}) collective-permute-start(bf16[64,1,160]{2,0,1:T(8,128)(2,1)S(1)} %get-tuple-element.6), channel_id=1, source_target_pairs={{16,0},{32,16},{48,32},{64,48},{80,64},{96,80},{112,96},{128,112},... | collective-permute-start | bytes 61448 | tf_op jit(solution)/shard_map/ppermute | solution.py:30
  73.6 6.8 %collective-permute-start.12 = (bf16[64,1,160]{2,0,1:T(8,128)(2,1)S(1)}, bf16[64,1,160]{2,0,1:T(8,128)(2,1)S(1)}, u32[]{:S(2)}, u32[]{:S(2)}) collective-permute-start(bf16[64,1,160]{2,0,1:T(8,128)(2,1)S(1)} %get-tuple-element.5), channel_id=1, source_target_pairs={{0,16},{16,32},{32,48},{48,64},{64,80},{80,96},{96,112},{112,128},... | collective-permute-start | bytes 61448 | tf_op jit(solution)/shard_map/ppermute | solution.py:29
  156.8 4.5 %copy-start.1 = (bf16[1024,2560]{1,0:T(8,128)(2,1)S(1)}, bf16[1024,2560]{1,0:T(8,128)(2,1)}, u32[]{:S(2)}) copy-start(bf16[1024,2560]{1,0:T(8,128)(2,1)} %all-gather.2.cloned.1.call-done) | copy-start | bytes 15728644
  197.0 23.9 %all-to-all-start.1 = ((f32[32,1,2080]{2,1,0:T(1,128)}), f32[32,1,2080]{2,1,0:T(1,128)S(1)}, u32[]{:S(2)}, u32[]{:S(2)}) async-start(f32[32,1,2080]{2,1,0:T(1,128)} %broadcast_in_dim.5), calls=%async_computation.1 | async-start | bytes 557056 | tf_op jit(solution)/shard_map/all_to_all | solution.py:59
Sparse Core Ops, SparseCore 0:
  82.8 73.9 all-gather.1
where the time goes:
time: 236 us; the launch traced here: 233 us
  waiting for transfers between devices  111 us (47%)
  starting transfers between devices  48 us (20%)
  blocking collectives  33.2 us (14%)
  matrix products  18.3 us (8%)
  between operations  13.8 us (6%)
  local copies, waits for them, and re-layouts  5.35 us (2%)
  other arithmetic  3.15 us (1%)
    all_gather x1, waiting for transfers between devices, shards(): every_band = lax.all_gather(filtered, 'band', axis=0, tiled=True)  74.1 us
    all_to_all x1, blocking collectives, sent_and_summed(): lax.all_to_all(pieces, axis, split_axis=0, concat_axis=0, tiled=True)  33.2 us
    ppermute x6, starting transfers between devices, with_halo(): before = lax.ppermute(last, axis, up)  21.3 us
    ppermute x6, starting transfers between devices, with_halo(): after = lax.ppermute(leading, axis, down)  20 us
    all_to_all x1, waiting for transfers between devices, from_everyone(): lax.all_to_all(jnp.broadcast_to(array[None], (count, *array.shape)), axis...  19.2 us
    ppermute x6, waiting for transfers between devices, with_halo(): before = lax.ppermute(last, axis, up)  14 us
  transfers between devices with their start and end apart: 15, of which 8 were waited for; matrix products, arithmetic and copies ran while one was open for 3% of the time, Pallas kernels for 0%

commit v1 on v0

v1 whole, which is shorter than its diff:
```python
import functools
import math

import jax
import jax.numpy as jnp
from jax import lax
from jax.experimental import pallas as pl
from jax.experimental.pallas import tpu as pltpu
from jax.sharding import PartitionSpec as P

MESH = pl.DeviceIdType.MESH
DEGREE = 6
CENTER = 0.4
HALF = 2.8
EPS = 1e-06
F32 = jnp.float32
BF16 = jnp.bfloat16

NB = 160
PAD = 256
NE = 8
ROWS = 128
HALFROWS = 64
COLS = NE * NB
ZL = 4
ZN = 16
XL = 2
NY = 4
CHIPS = 8
BANDS = ROWS * CHIPS


def nt_dot(a, b):
    return lax.dot_general(a, b, (((1,), (1,)), ((), ())), preferred_element_type=F32)


def kernel(
    total_rows,
    sizes,
    pattern,
    hd,
    hc,
    bands,
    out,
    wts,
    buf,
    dbuf,
    cbuf,
    csend,
    cprev,
    raw,
    fall,
    strip,
    s1,
    r1,
    s2,
    r2,
    s3,
    r3,
    s4,
    r4,
    sqs,
    sqr,
    wfull,
    obuf,
    local_sem,
    halo_send,
    halo_recv,
    gat_send,
    gat_recv,
    red_send,
    red_recv,
    sq_send,
    sq_recv,
):
    e = lax.axis_index("elem")
    b = lax.axis_index("band")
    ne = lax.axis_size("elem")
    core = b % 2
    other = 1 - core
    chip = b // 2
    xh = chip // NY
    y = chip % NY
    xl = e // ZN
    z = e % ZN
    zh = z // ZL
    zl = z % ZL

    def at(e_, b_):
        return (e_, b_)

    partner = at(e, chip * 2 + other)
    left = at((e + ne - other) % ne, chip * 2 + other)
    right = at((e + core) % ne, chip * 2 + other)
    xpeer = at(e, ((1 - xh) * NY + y) * 2 + core)
    yup = at(e, (xh * NY + (y + 1) % NY) * 2 + core)
    ydn = at(e, (xh * NY + (y + NY - 1) % NY) * 2 + core)
    xlpeer = at((1 - xl) * ZN + z, b)
    near = [at(xl * ZN + zh * ZL + (zl + j) % ZL, b) for j in range(1, ZL)]
    far = [at(xl * ZN + ((zh + j) % ZL) * ZL + zl, b) for j in range(1, ZL)]

    barrier = pltpu.get_barrier_semaphore()
    friends = [left, right, xpeer, yup, ydn, xlpeer] + near + far
    for who in friends:
        pl.semaphore_signal(barrier, inc=1, device_id=who, device_id_type=MESH)

    def remote(src, dst, ss, rs, who):
        return pltpu.make_async_remote_copy(
            src_ref=src, dst_ref=dst, send_sem=ss, recv_sem=rs, device_id=who, device_id_type=MESH
        )

    mine = pl.ds(pl.multiple_of(core * COLS, 128), COLS)
    theirs = pl.ds(pl.multiple_of(other * COLS, 128), COLS)
    my_rows = pl.ds(pl.multiple_of(core * HALFROWS, HALFROWS), HALFROWS)
    other_rows = pl.ds(pl.multiple_of(other * HALFROWS, HALFROWS), HALFROWS)
    my_elems = pl.ds(core * NE, NE)

    load_c = pltpu.make_async_copy(hc.at[my_elems], cbuf, local_sem.at[0])
    load_d = pltpu.make_async_copy(hd.at[my_elems], dbuf, local_sem.at[1])
    load_v = pltpu.make_async_copy(bands.at[:, mine], raw.at[my_rows], local_sem.at[2])
    load_c.start()
    load_v.start()
    load_d.start()

    def size_of(i):
        return sizes[core * NE + i]

    lanes_nb = lax.broadcasted_iota(jnp.int32, (NB, NB), 1)
    eye = (lax.broadcasted_iota(jnp.int32, (NB, NB), 0) == lanes_nb).astype(BF16)

    wts[...] = jnp.zeros_like(wts)
    load_c.wait()

    def coupled(i):
        on = jnp.full((NB, NB), pattern[core * NE + i], jnp.int32) != 0
        return jnp.where(on, cbuf[i].astype(F32), 0.0)

    csend[...] = coupled(NE - 1).astype(BF16)
    load_d.wait()
    for i in range(NE):
        keep = lanes_nb < size_of(i)
        wts[i, PAD : PAD + NB, 0:NB] = jnp.where(keep, dbuf[i].astype(F32), 0.0).astype(BF16)
        pc = coupled(i)
        turned = nt_dot(eye, pc.astype(BF16))
        wts[i, 2 * PAD : 2 * PAD + NB, 0:NB] = jnp.where(keep, turned, 0.0).astype(BF16)
        if i + 1 < NE:
            keep_next = lanes_nb < size_of(i + 1)
            wts[i + 1, 0:NB, 0:NB] = jnp.where(keep_next, pc, 0.0).astype(BF16)

    pl.semaphore_wait(barrier, len(friends))

    swap = remote(bands.at[:, theirs], raw.at[my_rows], gat_send.at[9], gat_recv.at[9], partner)
    swap.start()
    pass_c = remote(csend, cprev, gat_send.at[10], gat_recv.at[10], right)
    pass_c.start()

    def slot(i):
        return slice(PAD * i, PAD * (i + 1))

    def halo(m, side):
        v = buf.at[m % 2]
        if side == 0:
            src, dst, who = v.at[:, slot(1)], v.at[:, slot(NE + 1)], left
        else:
            src, dst, who = v.at[:, slot(NE)], v.at[:, slot(0)], right
        return remote(src, dst, halo_send.at[m % 2, side], halo_recv.at[m % 2, side], who)

    load_v.wait()
    swap.wait_recv()
    lanes_pad = lax.broadcasted_iota(jnp.int32, (ROWS, PAD), 1)

    def expand(i):
        start = (NB * i) // 128 * 128
        off = NB * i - start
        x = raw[:, start : start + PAD].astype(F32)
        if off:
            x = pltpu.roll(x, PAD - off, 1)
        buf[0, :, slot(i + 1)] = jnp.where(lanes_pad < size_of(i), x, 0.0).astype(BF16)

    expand(0)
    halo(0, 0).start()
    expand(NE - 1)
    halo(0, 1).start()
    for i in range(1, NE - 1):
        expand(i)
    pass_c.wait_recv()
    wts[0, 0:NB, 0:NB] = jnp.where(lanes_nb < size_of(0), cprev[...].astype(F32), 0.0).astype(BF16)

    def element(t, i):
        now, then = t % 2, (t + 1) % 2
        acc = jnp.dot(
            buf[now, :, PAD * i : PAD * (i + 3)], wts[i], preferred_element_type=F32
        )
        shifted = acc - CENTER * buf[now, :, slot(i + 1)].astype(F32)
        if t == 0:
            nxt = shifted * (1.0 / HALF)
        else:
            nxt = shifted * (2.0 / HALF) - buf[then, :, slot(i + 1)].astype(F32)
        buf[then, :, slot(i + 1)] = nxt.astype(BF16)

    for t in range(DEGREE):
        halo(t, 1).wait_recv()
        if t >= 1:
            halo(t - 1, 0).wait_send()
        element(t, 0)
        if t + 1 < DEGREE:
            halo(t + 1, 0).start()
        halo(t, 0).wait_recv()
        if t >= 1:
            halo(t - 1, 1).wait_send()
        element(t, NE - 1)
        if t + 1 < DEGREE:
            halo(t + 1, 1).start()
        for i in range(1, NE - 1):
            element(t, i)

    final = DEGREE % 2
    chunks = {}
    for i in range(NE):
        start = (NB * i) // 128
        off = NB * i - 128 * start
        x = buf[final, :, slot(i + 1)].astype(F32)
        if off:
            x = pltpu.roll(x, off, 1)
        for k in range(2):
            part = x[:, 128 * k : 128 * (k + 1)]
            at_chunk = start + k
            chunks[at_chunk] = chunks[at_chunk] + part if at_chunk in chunks else part
        done_to = COLS // 128 if i == NE - 1 else (NB * (i + 1)) // 128
        for c in sorted(chunks):
            if c < done_to:
                fall[chip, :, 128 * c : 128 * (c + 1)] = chunks.pop(c).astype(BF16)

    def block(h_, y_):
        return h_ * NY + y_

    y_up, y_dn, y_far = (y + 1) % NY, (y + NY - 1) % NY, (y + 2) % NY
    ox = 1 - xh
    low, high = slice(0, HALFROWS), slice(HALFROWS, ROWS)

    def gather(k, src, who):
        return remote(src, src, gat_send.at[k], gat_recv.at[k], who)

    own = fall.at[chip]
    sends = [gather(0, own, xpeer), gather(1, own, yup), gather(2, own, ydn)]
    for copy in sends:
        copy.start()

    r128 = lax.broadcasted_iota(jnp.int32, (ROWS, ROWS), 0)
    c128 = lax.broadcasted_iota(jnp.int32, (ROWS, ROWS), 1)
    r8 = lax.broadcasted_iota(jnp.int32, (CHIPS, ROWS), 0)
    mine_f = fall.at[chip]
    sqs[0] = jnp.zeros((CHIPS, ROWS), F32)

    def gram(g):
        there = fall[g]
        strip[:, pl.ds(pl.multiple_of(g * ROWS, ROWS), ROWS)] = nt_dot(mine_f[...], there)
        square = nt_dot(there, there)
        diag = jnp.sum(jnp.where(r128 == c128, square, 0.0), axis=0, keepdims=True)
        sqs[0] = jnp.where(r8 == g, diag, sqs[0])

    gram(chip)
    sends[1].wait_recv()
    sends.append(gather(3, fall.at[block(xh, y_dn), low], yup))
    sends[3].start()
    gram(block(xh, y_dn))
    sends[2].wait_recv()
    sends.append(gather(4, fall.at[block(xh, y_up), high], ydn))
    sends[4].start()
    gram(block(xh, y_up))
    sends[0].wait_recv()
    sends.append(gather(5, fall.at[block(ox, y)], yup))
    sends.append(gather(6, fall.at[block(ox, y)], ydn))
    sends[5].start()
    sends[6].start()
    gram(block(ox, y))
    sends[3].wait_recv()
    sends[4].wait_recv()
    gram(block(xh, y_far))
    sends[5].wait_recv()
    sends.append(gather(7, fall.at[block(ox, y_dn), low], yup))
    sends[7].start()
    gram(block(ox, y_dn))
    sends[6].wait_recv()
    sends.append(gather(8, fall.at[block(ox, y_up), high], ydn))
    sends[8].start()
    gram(block(ox, y_up))
    sends[7].wait_recv()
    sends[8].wait_recv()
    gram(block(ox, y_far))

    def stage(k, src, dst, who):
        return remote(src, dst, red_send.at[k], red_recv.at[k], who)

    def squares(k, s, who):
        return remote(sqs.at[s], sqr.at[k], sq_send.at[k], sq_recv.at[k], who)

    s1[...] = strip[other_rows, :].astype(BF16)
    copies = [stage(0, s1, r1, partner), squares(0, 0, partner)]
    for copy in copies:
        copy.start()
    for copy in copies:
        copy.wait_recv()
    half = strip.at[my_rows]
    half[...] = half[...] + r1[...].astype(F32)
    sqs[1] = sqs[0] + sqr[0]
    sends += copies

    quarter = HALFROWS // XL
    rest = strip.at[pl.ds(pl.multiple_of(core * HALFROWS + (1 - xl) * quarter, quarter), quarter)]
    row0 = pl.multiple_of(core * HALFROWS + xl * quarter, quarter)
    piece_rows = pl.ds(row0, quarter)
    s2[...] = rest[...].astype(BF16)
    copies = [stage(1, s2, r2, xlpeer), squares(1, 1, xlpeer)]
    for copy in copies:
        copy.start()
    for copy in copies:
        copy.wait_recv()
    piece = strip.at[piece_rows]
    total = piece[...] + r2[...].astype(F32)
    piece[...] = total
    s3[...] = total.astype(BF16)
    sqs[2] = sqs[1] + sqr[1]
    sends += copies

    width = BANDS // ZL
    my_cols = pl.ds(pl.multiple_of(zl * width, width), width)
    copies = []
    for j in range(1, ZL):
        cols = pl.ds(pl.multiple_of(((zl + j) % ZL) * width, width), width)
        copies.append(stage(1 + j, s3.at[:, cols], r3.at[j - 1], near[j - 1]))
        copies.append(squares(1 + j, 2, near[j - 1]))
    for copy in copies:
        copy.start()
    for copy in copies:
        copy.wait_recv()
    total = piece[:, my_cols]
    sq = sqs[2]
    for j in range(1, ZL):
        total = total + r3[j - 1].astype(F32)
        sq = sq + sqr[1 + j]
    s4[...] = total.astype(BF16)
    sqs[3] = sq
    sends += copies

    copies = []
    for j in range(1, ZL):
        copies.append(stage(4 + j, s4, r4.at[j - 1], far[j - 1]))
        copies.append(squares(4 + j, 3, far[j - 1]))
    for copy in copies:
        copy.start()
    for copy in copies:
        copy.wait_recv()
    for j in range(1, ZL):
        total = total + r4[j - 1].astype(F32)
        sq = sq + sqr[4 + j]
    sends += copies

    scale = lax.rsqrt(sq + EPS)
    ri = lax.broadcasted_iota(jnp.int32, (quarter, ROWS), 0) + row0
    ci = lax.broadcasted_iota(jnp.int32, (quarter, ROWS), 1)
    same = ri == ci

    def row_of(table, g):
        return jnp.sum(jnp.where(r8 == g, table, 0.0), axis=0, keepdims=True)

    own_scale = jnp.sum(jnp.where(same, row_of(scale, chip), 0.0), axis=1, keepdims=True)
    for k in range(width // ROWS):
        g = zl * (width // ROWS) + k
        scale_row = row_of(scale, g)
        unit = jnp.logical_and(same, jnp.full(same.shape, g - chip, jnp.int32) == 0)
        value = total[:, ROWS * k : ROWS * (k + 1)]
        value = jnp.where(unit, row_of(sq, g), value)
        normed = own_scale * value * scale_row
        w = math.sqrt(total_rows) * scale_row * (jnp.where(unit, 1.5, 0.0) - 0.5 * normed)
        wfull[piece_rows, pl.ds(pl.multiple_of(g * ROWS, ROWS), ROWS)] = w.astype(BF16)

    mine_w = wfull.at[piece_rows, my_cols]
    copies = [stage(7 + j, mine_w, mine_w, near[j - 1]) for j in range(1, ZL)]
    for copy in copies:
        copy.start()
    for copy in copies:
        copy.wait_recv()
    sends += copies
    mine_w = wfull.at[piece_rows]
    copy = stage(11, mine_w, mine_w, xlpeer)
    copy.start()
    copy.wait_recv()
    sends.append(copy)
    mine_w = wfull.at[my_rows]
    copy = stage(12, mine_w, mine_w, partner)
    copy.start()
    copy.wait_recv()
    sends.append(copy)

    whole = fall.reshape(BANDS, COLS)
    for k in range(COLS // PAD):
        obuf[:, PAD * k : PAD * (k + 1)] = jnp.dot(
            wfull[...], whole[:, PAD * k : PAD * (k + 1)], preferred_element_type=F32
        ).astype(BF16)
    give = remote(
        obuf.at[other_rows], out.at[:, mine], gat_send.at[11], gat_recv.at[11], partner
    )
    give.start()
    keep_own = pltpu.make_async_copy(obuf.at[my_rows], out.at[:, mine], local_sem.at[3])
    keep_own.start()
    for copy in sends:
        copy.wait_send()
    swap.wait_send()
    pass_c.wait_send()
    halo(DEGREE - 1, 0).wait_send()
    halo(DEGREE - 1, 1).wait_send()
    keep_own.wait()
    give.wait()


def shards(basis_sizes, coupling_pattern, h_diag, h_couple, bands):
    total_rows = h_diag.shape[0] * lax.axis_size("elem") * h_diag.shape[1]
    smem = pl.BlockSpec(memory_space=pltpu.SMEM)
    hbm = pl.BlockSpec(memory_space=pl.ANY)
    dma = pltpu.SemaphoreType.DMA
    quarter = HALFROWS // XL
    width = BANDS // ZL
    return pl.pallas_call(
        functools.partial(kernel, total_rows),
        out_shape=jax.ShapeDtypeStruct(bands.shape, BF16),
        in_specs=[smem, smem, hbm, hbm, hbm],
        out_specs=hbm,
        scratch_shapes=[
            pltpu.VMEM((NE, 3 * PAD, PAD), BF16),
            pltpu.VMEM((2, ROWS, PAD * (NE + 2)), BF16),
            pltpu.VMEM((NE, NB, NB), BF16),
            pltpu.VMEM((NE, NB, NB), BF16),
            pltpu.VMEM((NB, NB), BF16),
            pltpu.VMEM((NB, NB), BF16),
            pltpu.VMEM((ROWS, COLS), BF16),
            pltpu.VMEM((CHIPS, ROWS, COLS), BF16),
            pltpu.VMEM((ROWS, BANDS), F32),
            pltpu.VMEM((HALFROWS, BANDS), BF16),
            pltpu.VMEM((HALFROWS, BANDS), BF16),
            pltpu.VMEM((quarter, BANDS), BF16),
            pltpu.VMEM((quarter, BANDS), BF16),
            pltpu.VMEM((quarter, BANDS), BF16),
            pltpu.VMEM((ZL - 1, quarter, width), BF16),
            pltpu.VMEM((quarter, width), BF16),
            pltpu.VMEM((ZL - 1, quarter, width), BF16),
            pltpu.VMEM((4, CHIPS, ROWS), F32),
            pltpu.VMEM((8, CHIPS, ROWS), F32),
            pltpu.VMEM((ROWS, BANDS), BF16),
            pltpu.VMEM((ROWS, COLS), BF16),
            dma((4,)),
            dma((2, 2)),
            dma((2, 2)),
            dma((12,)),
            dma((12,)),
            dma((13,)),
            dma((13,)),
            dma((8,)),
            dma((8,)),
        ],
        compiler_params=pltpu.CompilerParams(
            collective_id=0, has_side_effects=True, vmem_limit_bytes=40 * 1024 * 1024
        ),
        name="filter_step",
    )(basis_sizes, coupling_pattern, h_diag, h_couple, bands)


def solution(mesh):
    in_specs = (
        P("elem"),
        P("elem"),
        P("elem", None, None),
        P("elem", None, None),
        P("band", "elem"),
    )
    out_specs = P("band", "elem")
    return jax.shard_map(shards, mesh=mesh, in_specs=in_specs, out_specs=out_specs, check_vma=False)
```

time: 236 us -> 99.4 us (0.42); the launches traced: 233 us -> 99.2 us
  waiting for transfers between devices: 111 us -> 0 us
  Pallas kernels: 0 us -> 93.5 us
  starting transfers between devices: 48 us -> 0 us
  blocking collectives: 33.2 us -> 0 us
  matrix products: 18.3 us -> 0 us
  between operations: 13.8 us -> 0.01 us
  other arithmetic: 3.15 us -> 0 us
    pallas_call x0 -> x1, Pallas kernels: none -> 93.5 us  [shards(): pl.pallas_call(functools.partial(kernel, total_rows), out_shape=jax.Shape...]
    all_gather x1 -> x0, waiting for transfers between devices: 74.1 us -> none  [shards(): every_band = lax.all_gather(filtered, 'band', axis=0, tiled=True)]
    ppermute x13 -> x0, starting transfers between devices: 43.3 us -> none  [the longest x6 21.3 us: with_halo(): before = lax.ppermute(last, axis, up)]
    all_to_all x1 -> x0, blocking collectives: 33.2 us -> none  [sent_and_summed(): lax.all_to_all(pieces, axis, split_axis=0, concat_axis=0, tiled=True)]
    all_to_all x1 -> x0, waiting for transfers between devices: 19.2 us -> none  [from_everyone(): lax.all_to_all(jnp.broadcast_to(array[None], (count, *array.shape)), axis...]
    dot_general x20 -> x0, matrix products: 18.3 us -> none  [the longest x1 4.42 us: shards(): lax.dot_general(filtered, every_band, (((1,), (1,)), ((), ())), preferred...]
    ppermute x13 -> x0, waiting for transfers between devices: 18.2 us -> none  [the longest x6 14 us: with_halo(): before = lax.ppermute(last, axis, up)]
    unnamed x9 -> x11, local copies, waits for them, and re-layouts: 0.07 us -> 5.64 us
  transfers between devices with their start and end apart: 15 -> 0, of which waited for: 8 -> 0; matrix products, arithmetic and copies ran while one was open for 3% -> 0% of each run, Pallas kernels for 0% -> 0%
where the time goes in v1:
time: 99.4 us; the launch traced here: 99.2 us
  Pallas kernels  93.5 us (94%)
  local copies, waits for them, and re-layouts  5.64 us (6%)
    pallas_call x1, Pallas kernels, shards(): pl.pallas_call(functools.partial(kernel, total_rows), out_shape=jax.Shape...  93.5 us
    unnamed x11, local copies, waits for them, and re-layouts  5.64 us

profile of v1, /device:TPU:1, one launch (start us, length us, event | category | flops | bytes accessed | tf_op | source)
XLA Modules:
  0.0 99.2 jit_solution(15313667706535044567)
XLA Ops:
  0.0 0.0 copy-start
  0.0 1.3 %copy-done = bf16[16,160,160]{2,1,0:T(8,128)(2,1)S(1)} copy-done((bf16[16,160,160]{2,1,0:T(8,128)(2,1)S(1)}, bf16[16,160,160]{2,1,0:T(8,128)(2,1)}, u32[]{:S(2)}) %copy-start) | copy-done | bytes 819224
  1.3 0.0 copy-start.1
  1.3 1.3 %copy-done.1 = bf16[16,160,160]{2,1,0:T(8,128)(2,1)S(1)} copy-done((bf16[16,160,160]{2,1,0:T(8,128)(2,1)S(1)}, bf16[16,160,160]{2,1,0:T(8,128)(2,1)}, u32[]{:S(2)}) %copy-start.1) | copy-done | bytes 819224
  2.6 0.0 copy-start.2
  2.6 1.0 copy-done.2
  3.6 0.0 copy-start.3
  3.6 0.7 copy-done.3
  4.3 0.0 copy-start.4
  4.3 0.7 copy-done.4
  4.9 93.5 %filter_step.1 = bf16[64,2560]{1,0:T(8,128)(2,1)S(1)} custom-call(s32[16]{0:T(128)S(1)} %copy-done.3, s32[16]{0:T(128)S(1)} %copy-done.4, bf16[16,160,160]{2,1,0:T(8,128)(2,1)S(1)} %copy-done, bf16[16,160,160]{2,1,0:T(8,128)(2,1)S(1)} %copy-done.1, bf16[64,2560]{1,0:T(8,128)(2,1)S(1)} %copy-done.2), custom_call_target="tpu_custom_call" | custom-call | tf_op jit(solution)/shard_map/filter_step/pallas_call | solution.py:424
  98.4 0.7 copy.7
Async XLA Ops:
  0.0 1.3 %copy-start = (bf16[16,160,160]{2,1,0:T(8,128)(2,1)S(1)}, bf16[16,160,160]{2,1,0:T(8,128)(2,1)}, u32[]{:S(2)}) copy-start(bf16[16,160,160]{2,1,0:T(8,128)(2,1)} %hd.1) | copy-start | bytes 2457604
  1.3 1.3 %copy-start.1 = (bf16[16,160,160]{2,1,0:T(8,128)(2,1)S(1)}, bf16[16,160,160]{2,1,0:T(8,128)(2,1)}, u32[]{:S(2)}) copy-start(bf16[16,160,160]{2,1,0:T(8,128)(2,1)} %hc.1) | copy-start | bytes 2457604
  2.6 1.0 copy-start.2
  3.6 0.7 copy-start.3
  4.3 0.7 copy-start.4

commit v2 on v1

--- a/solution.py
+++ b/solution.py
@@ -28,6 +28,7 @@
 NY = 4
 CHIPS = 8
 BANDS = ROWS * CHIPS
+SIDE = ROWS * NY
 
 
 def nt_dot(a, b):
@@ -36,8 +37,8 @@
 
 def kernel(
     total_rows,
-    sizes,
-    pattern,
+    sizes_hbm,
+    pattern_hbm,
     hd,
     hc,
     bands,
@@ -58,11 +59,12 @@
     s3,
     r3,
     s4,
-    r4,
     sqs,
     sqr,
     wfull,
     obuf,
+    sizes,
+    pattern,
     local_sem,
     halo_send,
     halo_recv,
@@ -95,12 +97,13 @@
     xpeer = at(e, ((1 - xh) * NY + y) * 2 + core)
     yup = at(e, (xh * NY + (y + 1) % NY) * 2 + core)
     ydn = at(e, (xh * NY + (y + NY - 1) % NY) * 2 + core)
-    xlpeer = at((1 - xl) * ZN + z, b)
-    near = [at(xl * ZN + zh * ZL + (zl + j) % ZL, b) for j in range(1, ZL)]
+    places = [((xl + j // ZL) % XL) * ZN + zh * ZL + (zl + j) % ZL for j in range(XL * ZL)]
+    near = [at(p, b) for p in places[1:]]
+    across = [at(p, xpeer[1]) for p in places]
     far = [at(xl * ZN + ((zh + j) % ZL) * ZL + zl, b) for j in range(1, ZL)]
 
     barrier = pltpu.get_barrier_semaphore()
-    friends = [left, right, xpeer, yup, ydn, xlpeer] + near + far
+    friends = [left, right, yup, ydn] + near + across + far
     for who in friends:
         pl.semaphore_signal(barrier, inc=1, device_id=who, device_id_type=MESH)
 
@@ -118,9 +121,10 @@
     load_c = pltpu.make_async_copy(hc.at[my_elems], cbuf, local_sem.at[0])
     load_d = pltpu.make_async_copy(hd.at[my_elems], dbuf, local_sem.at[1])
     load_v = pltpu.make_async_copy(bands.at[:, mine], raw.at[my_rows], local_sem.at[2])
-    load_c.start()
-    load_v.start()
-    load_d.start()
+    load_s = pltpu.make_async_copy(sizes_hbm, sizes, local_sem.at[5])
+    load_p = pltpu.make_async_copy(pattern_hbm, pattern, local_sem.at[6])
+    for load in (load_s, load_p, load_c, load_d, load_v):
+        load.start()
 
     def size_of(i):
         return sizes[core * NE + i]
@@ -129,6 +133,8 @@
     eye = (lax.broadcasted_iota(jnp.int32, (NB, NB), 0) == lanes_nb).astype(BF16)
 
     wts[...] = jnp.zeros_like(wts)
+    load_s.wait()
+    load_p.wait()
     load_c.wait()
 
     def coupled(i):
@@ -231,11 +237,9 @@
             if c < done_to:
                 fall[chip, :, 128 * c : 128 * (c + 1)] = chunks.pop(c).astype(BF16)
 
-    def block(h_, y_):
-        return h_ * NY + y_
-
     y_up, y_dn, y_far = (y + 1) % NY, (y + NY - 1) % NY, (y + 2) % NY
-    ox = 1 - xh
+    peer_chip = (1 - xh) * NY + y
+    side, far_side = xh * NY, (1 - xh) * NY
     low, high = slice(0, HALFROWS), slice(HALFROWS, ROWS)
 
     def gather(k, src, who):
@@ -249,45 +253,44 @@
     r128 = lax.broadcasted_iota(jnp.int32, (ROWS, ROWS), 0)
     c128 = lax.broadcasted_iota(jnp.int32, (ROWS, ROWS), 1)
     r8 = lax.broadcasted_iota(jnp.int32, (CHIPS, ROWS), 0)
-    mine_f = fall.at[chip]
     sqs[0] = jnp.zeros((CHIPS, ROWS), F32)
 
-    def gram(g):
+    def cols_of(y_):
+        return pl.ds(pl.multiple_of(y_ * ROWS, ROWS), ROWS)
+
+    def norms(g):
         there = fall[g]
-        strip[:, pl.ds(pl.multiple_of(g * ROWS, ROWS), ROWS)] = nt_dot(mine_f[...], there)
         square = nt_dot(there, there)
         diag = jnp.sum(jnp.where(r128 == c128, square, 0.0), axis=0, keepdims=True)
         sqs[0] = jnp.where(r8 == g, diag, sqs[0])
 
-    gram(chip)
+    def gram(part, g, y_):
+        strip[part, :, cols_of(y_)] = nt_dot(fall[g], fall[side + y_])
+
+    gram(0, chip, y)
+    norms(chip)
     sends[1].wait_recv()
-    sends.append(gather(3, fall.at[block(xh, y_dn), low], yup))
+    sends.append(gather(3, fall.at[side + y_dn, low], yup))
     sends[3].start()
-    gram(block(xh, y_dn))
+    gram(0, chip, y_dn)
+    norms(side + y_dn)
     sends[2].wait_recv()
-    sends.append(gather(4, fall.at[block(xh, y_up), high], ydn))
+    sends.append(gather(4, fall.at[side + y_up, high], ydn))
     sends[4].start()
-    gram(block(xh, y_up))
+    gram(0, chip, y_up)
+    norms(side + y_up)
+    sends[3].wait_recv()
+    sends[4].wait_recv()
+    gram(0, chip, y_far)
+    norms(side + y_far)
     sends[0].wait_recv()
-    sends.append(gather(5, fall.at[block(ox, y)], yup))
-    sends.append(gather(6, fall.at[block(ox, y)], ydn))
+    sends.append(gather(5, fall.at[peer_chip], yup))
+    sends.append(gather(6, fall.at[peer_chip], ydn))
     sends[5].start()
     sends[6].start()
-    gram(block(ox, y))
-    sends[3].wait_recv()
-    sends[4].wait_recv()
-    gram(block(xh, y_far))
-    sends[5].wait_recv()
-    sends.append(gather(7, fall.at[block(ox, y_dn), low], yup))
-    sends[7].start()
-    gram(block(ox, y_dn))
-    sends[6].wait_recv()
-    sends.append(gather(8, fall.at[block(ox, y_up), high], ydn))
-    sends[8].start()
-    gram(block(ox, y_up))
-    sends[7].wait_recv()
-    sends[8].wait_recv()
-    gram(block(ox, y_far))
+    for y_ in range(NY):
+        gram(1, peer_chip, y_)
+    norms(peer_chip)
 
     def stage(k, src, dst, who):
         return remote(src, dst, red_send.at[k], red_recv.at[k], who)
@@ -295,101 +298,97 @@
     def squares(k, s, who):
         return remote(sqs.at[s], sqr.at[k], sq_send.at[k], sq_recv.at[k], who)
 
-    s1[...] = strip[other_rows, :].astype(BF16)
+    s1[...] = strip[:, other_rows, :].astype(BF16)
     copies = [stage(0, s1, r1, partner), squares(0, 0, partner)]
     for copy in copies:
         copy.start()
     for copy in copies:
         copy.wait_recv()
-    half = strip.at[my_rows]
-    half[...] = half[...] + r1[...].astype(F32)
+    half = strip[:, my_rows, :] + r1[...].astype(F32)
+    strip[:, my_rows, :] = half
+    s2[...] = half.astype(BF16)
     sqs[1] = sqs[0] + sqr[0]
     sends += copies
 
     quarter = HALFROWS // XL
-    rest = strip.at[pl.ds(pl.multiple_of(core * HALFROWS + (1 - xl) * quarter, quarter), quarter)]
+    copies = []
+    for j in range(1, XL * ZL):
+        xl_, zl_ = (xl + j // ZL) % XL, (zl + j) % ZL
+        rows = pl.ds(pl.multiple_of(xl_ * quarter, quarter), quarter)
+        copies.append(stage(j, s2.at[:, rows, cols_of(zl_)], r2.at[j - 1], near[j - 1]))
+        copies.append(squares(j, 1, near[j - 1]))
+    for copy in copies:
+        copy.start()
     row0 = pl.multiple_of(core * HALFROWS + xl * quarter, quarter)
     piece_rows = pl.ds(row0, quarter)
-    s2[...] = rest[...].astype(BF16)
-    copies = [stage(1, s2, r2, xlpeer), squares(1, 1, xlpeer)]
-    for copy in copies:
-        copy.start()
+    total = strip[:, piece_rows, cols_of(zl)]
+    sq = sqs[1]
     for copy in copies:
         copy.wait_recv()
-    piece = strip.at[piece_rows]
-    total = piece[...] + r2[...].astype(F32)
-    piece[...] = total
+    for j in range(1, XL * ZL):
+        total = total + r2[j - 1].astype(F32)
+        sq = sq + sqr[j]
     s3[...] = total.astype(BF16)
-    sqs[2] = sqs[1] + sqr[1]
+    sqs[2] = sq
     sends += copies
 
-    width = BANDS // ZL
-    my_cols = pl.ds(pl.multiple_of(zl * width, width), width)
     copies = []
     for j in range(1, ZL):
-        cols = pl.ds(pl.multiple_of(((zl + j) % ZL) * width, width), width)
-        copies.append(stage(1 + j, s3.at[:, cols], r3.at[j - 1], near[j - 1]))
-        copies.append(squares(1 + j, 2, near[j - 1]))
+        copies.append(stage(7 + j, s3, r3.at[j - 1], far[j - 1]))
+        copies.append(squares(7 + j, 2, far[j - 1]))
     for copy in copies:
         copy.start()
+    sends[5].wait_recv()
+    late = [gather(7, fall.at[far_side + y_dn, low], yup)]
+    late[0].start()
+    sends[6].wait_recv()
+    late.append(gather(8, fall.at[far_side + y_up, high], ydn))
+    late[1].start()
     for copy in copies:
         copy.wait_recv()
-    total = piece[:, my_cols]
-    sq = sqs[2]
     for j in range(1, ZL):
         total = total + r3[j - 1].astype(F32)
-        sq = sq + sqr[1 + j]
-    s4[...] = total.astype(BF16)
-    sqs[3] = sq
-    sends += copies
-
-    copies = []
-    for j in range(1, ZL):
-        copies.append(stage(4 + j, s4, r4.at[j - 1], far[j - 1]))
-        copies.append(squares(4 + j, 3, far[j - 1]))
-    for copy in copies:
-        copy.start()
-    for copy in copies:
-        copy.wait_recv()
-    for j in range(1, ZL):
-        total = total + r4[j - 1].astype(F32)
-        sq = sq + sqr[4 + j]
-    sends += copies
+        sq = sq + sqr[7 + j]
+    sends += copies + late
 
     scale = lax.rsqrt(sq + EPS)
     ri = lax.broadcasted_iota(jnp.int32, (quarter, ROWS), 0) + row0
     ci = lax.broadcasted_iota(jnp.int32, (quarter, ROWS), 1)
     same = ri == ci
-
-    def row_of(table, g):
-        return jnp.sum(jnp.where(r8 == g, table, 0.0), axis=0, keepdims=True)
-
-    own_scale = jnp.sum(jnp.where(same, row_of(scale, chip), 0.0), axis=1, keepdims=True)
-    for k in range(width // ROWS):
-        g = zl * (width // ROWS) + k
-        scale_row = row_of(scale, g)
-        unit = jnp.logical_and(same, jnp.full(same.shape, g - chip, jnp.int32) == 0)
-        value = total[:, ROWS * k : ROWS * (k + 1)]
-        value = jnp.where(unit, row_of(sq, g), value)
-        normed = own_scale * value * scale_row
-        w = math.sqrt(total_rows) * scale_row * (jnp.where(unit, 1.5, 0.0) - 0.5 * normed)
-        wfull[piece_rows, pl.ds(pl.multiple_of(g * ROWS, ROWS), ROWS)] = w.astype(BF16)
-
-    mine_w = wfull.at[piece_rows, my_cols]
-    copies = [stage(7 + j, mine_w, mine_w, near[j - 1]) for j in range(1, ZL)]
+    g = side + zl
+    scale_row = jnp.sum(jnp.where(r8 == g, scale, 0.0), axis=0, keepdims=True)
+    sq_row = jnp.sum(jnp.where(r8 == g, sq, 0.0), axis=0, keepdims=True)
+    for part in range(2):
+        of = chip if part == 0 else peer_chip
+        lanes = jnp.sum(jnp.where(r8 == of, scale, 0.0), axis=0, keepdims=True)
+        row_scale = jnp.sum(jnp.where(same, lanes, 0.0), axis=1, keepdims=True)
+        value = total[part]
+        ident = jnp.zeros_like(value)
+        if part == 0:
+            unit = jnp.logical_and(same, jnp.full(same.shape, zl - y, jnp.int32) == 0)
+            value = jnp.where(unit, sq_row, value)
+            ident = jnp.where(unit, 1.5, 0.0)
+        normed = row_scale * value * scale_row
+        w = math.sqrt(total_rows) * scale_row * (ident - 0.5 * normed)
+        s4[part] = w.astype(BF16)
+
+    g_cols = pl.ds(pl.multiple_of(g * ROWS, ROWS), ROWS)
+    place = wfull.at[piece_rows, g_cols]
+    put = pltpu.make_async_copy(s4.at[0], place, local_sem.at[4])
+    put.start()
+    copies = [stage(10 + j, s4.at[0], place, near[j - 1]) for j in range(1, XL * ZL)]
+    copies += [stage(18 + j, s4.at[1], place, across[j]) for j in range(XL * ZL)]
     for copy in copies:
         copy.start()
     for copy in copies:
         copy.wait_recv()
+    put.wait()
     sends += copies
-    mine_w = wfull.at[piece_rows]
-    copy = stage(11, mine_w, mine_w, xlpeer)
+    mine_w = wfull.at[my_rows]
+    copy = stage(26, mine_w, mine_w, partner)
     copy.start()
-    copy.wait_recv()
-    sends.append(copy)
-    mine_w = wfull.at[my_rows]
-    copy = stage(12, mine_w, mine_w, partner)
-    copy.start()
+    for waiting in late:
+        waiting.wait_recv()
     copy.wait_recv()
     sends.append(copy)
 
@@ -416,15 +415,13 @@
 
 def shards(basis_sizes, coupling_pattern, h_diag, h_couple, bands):
     total_rows = h_diag.shape[0] * lax.axis_size("elem") * h_diag.shape[1]
-    smem = pl.BlockSpec(memory_space=pltpu.SMEM)
-    hbm = pl.BlockSpec(memory_space=pl.ANY)
+    hbm = pl.BlockSpec(memory_space=pltpu.HBM)
     dma = pltpu.SemaphoreType.DMA
     quarter = HALFROWS // XL
-    width = BANDS // ZL
     return pl.pallas_call(
         functools.partial(kernel, total_rows),
         out_shape=jax.ShapeDtypeStruct(bands.shape, BF16),
-        in_specs=[smem, smem, hbm, hbm, hbm],
+        in_specs=[hbm] * 5,
         out_specs=hbm,
         scratch_shapes=[
             pltpu.VMEM((NE, 3 * PAD, PAD), BF16),
@@ -435,31 +432,32 @@
             pltpu.VMEM((NB, NB), BF16),
             pltpu.VMEM((ROWS, COLS), BF16),
             pltpu.VMEM((CHIPS, ROWS, COLS), BF16),
-            pltpu.VMEM((ROWS, BANDS), F32),
-            pltpu.VMEM((HALFROWS, BANDS), BF16),
-            pltpu.VMEM((HALFROWS, BANDS), BF16),
-            pltpu.VMEM((quarter, BANDS), BF16),
-            pltpu.VMEM((quarter, BANDS), BF16),
-            pltpu.VMEM((quarter, BANDS), BF16),
-            pltpu.VMEM((ZL - 1, quarter, width), BF16),
-            pltpu.VMEM((quarter, width), BF16),
-            pltpu.VMEM((ZL - 1, quarter, width), BF16),
-            pltpu.VMEM((4, CHIPS, ROWS), F32),
-            pltpu.VMEM((8, CHIPS, ROWS), F32),
+            pltpu.VMEM((2, ROWS, SIDE), F32),
+            pltpu.VMEM((2, HALFROWS, SIDE), BF16),
+            pltpu.VMEM((2, HALFROWS, SIDE), BF16),
+            pltpu.VMEM((2, HALFROWS, SIDE), BF16),
+            pltpu.VMEM((XL * ZL - 1, 2, quarter, ROWS), BF16),
+            pltpu.VMEM((2, quarter, ROWS), BF16),
+            pltpu.VMEM((ZL - 1, 2, quarter, ROWS), BF16),
+            pltpu.VMEM((2, quarter, ROWS), BF16),
+            pltpu.VMEM((3, CHIPS, ROWS), F32),
+            pltpu.VMEM((11, CHIPS, ROWS), F32),
             pltpu.VMEM((ROWS, BANDS), BF16),
             pltpu.VMEM((ROWS, COLS), BF16),
-            dma((4,)),
+            pltpu.SMEM((2 * NE,), jnp.int32),
+            pltpu.SMEM((2 * NE,), jnp.int32),
+            dma((7,)),
             dma((2, 2)),
             dma((2, 2)),
             dma((12,)),
             dma((12,)),
-            dma((13,)),
-            dma((13,)),
-            dma((8,)),
-            dma((8,)),
+            dma((27,)),
+            dma((27,)),
+            dma((11,)),
+            dma((11,)),
         ],
         compiler_params=pltpu.CompilerParams(
-            collective_id=0, has_side_effects=True, vmem_limit_bytes=40 * 1024 * 1024
+            collective_id=0, has_side_effects=True, vmem_limit_bytes=67043328
         ),
         name="filter_step",
     )(basis_sizes, coupling_pattern, h_diag, h_couple, bands)

time: 99.4 us -> 82.1 us (0.83)
  Pallas kernels: 93.5 us -> 80.2 us
  local copies, waits for them, and re-layouts: 5.64 us -> 1.72 us
    pallas_call x1, Pallas kernels: 93.5 us -> 80.2 us  [shards(): pl.pallas_call(functools.partial(kernel, total_rows), out_shape=jax.Shape...]
    unnamed x11 -> x1, local copies, waits for them, and re-layouts: 5.64 us -> 1.72 us
where the time goes in v2:
time: 82.1 us; the launch traced here: 82 us
  Pallas kernels  80.2 us (98%)
  local copies, waits for them, and re-layouts  1.72 us (2%)
    pallas_call x1, Pallas kernels, shards(): pl.pallas_call(functools.partial(kernel, total_rows), out_shape=jax.Shape...  80.2 us
    unnamed x1, local copies, waits for them, and re-layouts  1.72 us

profile of v2, /device:TPU:1, one launch (start us, length us, event | category | flops | bytes accessed | tf_op | source)
XLA Modules:
  0.0 82.0 jit_solution(15273433463273141621)
XLA Ops:
  0.0 80.2 %filter_step.1 = bf16[64,2560]{1,0:T(8,128)(2,1)} custom-call(s32[16]{0:T(128)} %sizes_hbm.1, s32[16]{0:T(128)} %pattern_hbm.1, bf16[16,160,160]{2,1,0:T(8,128)(2,1)} %hd.1, bf16[16,160,160]{2,1,0:T(8,128)(2,1)} %hc.1, bf16[64,2560]{1,0:T(8,128)(2,1)} %bands.1), custom_call_target="tpu_custom_call" | custom-call | tf_op jit(solution)/shard_map/filter_step/pallas_call | solution.py:421
  80.2 1.7 %copy.7 = bf16[64,2560]{1,0:T(8,128)(2,1)} copy(bf16[64,2560]{1,0:T(8,128)(2,1)} %filter_step.1) | data formatting | bytes 655360

commit v3 on v2

--- a/solution.py
+++ b/solution.py
@@ -22,6 +22,8 @@
 ROWS = 128
 HALFROWS = 64
 COLS = NE * NB
+DEEP = 3
+EDGE = 512
 ZL = 4
 ZN = 16
 XL = 2
@@ -47,9 +49,8 @@
     buf,
     dbuf,
     cbuf,
-    csend,
-    cprev,
     raw,
+    edges,
     fall,
     strip,
     s1,
@@ -65,9 +66,13 @@
     obuf,
     sizes,
     pattern,
+    sizes_left,
+    pattern_left,
+    sizes_right,
+    pattern_right,
     local_sem,
-    halo_send,
-    halo_recv,
+    ext_send,
+    ext_recv,
     gat_send,
     gat_recv,
     red_send,
@@ -118,114 +123,187 @@
     other_rows = pl.ds(pl.multiple_of(other * HALFROWS, HALFROWS), HALFROWS)
     my_elems = pl.ds(core * NE, NE)
 
-    load_c = pltpu.make_async_copy(hc.at[my_elems], cbuf, local_sem.at[0])
-    load_d = pltpu.make_async_copy(hd.at[my_elems], dbuf, local_sem.at[1])
+    own_c, own_d = slice(DEEP, DEEP + NE), slice(DEEP - 1, DEEP - 1 + NE)
+    load_c = pltpu.make_async_copy(hc.at[my_elems], cbuf.at[own_c], local_sem.at[0])
+    load_d = pltpu.make_async_copy(hd.at[my_elems], dbuf.at[own_d], local_sem.at[1])
     load_v = pltpu.make_async_copy(bands.at[:, mine], raw.at[my_rows], local_sem.at[2])
     load_s = pltpu.make_async_copy(sizes_hbm, sizes, local_sem.at[5])
     load_p = pltpu.make_async_copy(pattern_hbm, pattern, local_sem.at[6])
     for load in (load_s, load_p, load_c, load_d, load_v):
         load.start()
 
+    def number(own_table, left_table, right_table, i):
+        if i < 0:
+            return left_table[other * NE + NE + i]
+        if i >= NE:
+            return right_table[other * NE + i - NE]
+        return own_table[core * NE + i]
+
     def size_of(i):
-        return sizes[core * NE + i]
+        return number(sizes, sizes_left, sizes_right, i)
+
+    def slot(i, n=1):
+        return slice(PAD * (i + DEEP), PAD * (i + DEEP + n))
 
     lanes_nb = lax.broadcasted_iota(jnp.int32, (NB, NB), 1)
     eye = (lax.broadcasted_iota(jnp.int32, (NB, NB), 0) == lanes_nb).astype(BF16)
 
+    def coupled(i):
+        on = jnp.full((NB, NB), number(pattern, pattern_left, pattern_right, i), jnp.int32) != 0
+        return jnp.where(on, cbuf[i + DEEP].astype(F32), 0.0)
+
+    def put_weights(i, row, value):
+        keep = lanes_nb < size_of(i)
+        at_row = slice(row * PAD, row * PAD + NB)
+        wts[i + DEEP - 1, at_row, 0:NB] = jnp.where(keep, value, 0.0).astype(BF16)
+
+    def use_coupling(i):
+        pc = coupled(i)
+        if -DEEP + 1 <= i:
+            put_weights(i, 2, nt_dot(eye, pc.astype(BF16)))
+        if i + 1 < NE + DEEP - 1:
+            put_weights(i + 1, 0, pc)
+
+    def use_diagonal(i):
+        put_weights(i, 1, dbuf[i + DEEP - 1].astype(F32))
+
     wts[...] = jnp.zeros_like(wts)
-    load_s.wait()
-    load_p.wait()
-    load_c.wait()
-
-    def coupled(i):
-        on = jnp.full((NB, NB), pattern[core * NE + i], jnp.int32) != 0
-        return jnp.where(on, cbuf[i].astype(F32), 0.0)
-
-    csend[...] = coupled(NE - 1).astype(BF16)
-    load_d.wait()
+    for load in (load_s, load_p, load_c, load_d):
+        load.wait()
     for i in range(NE):
-        keep = lanes_nb < size_of(i)
-        wts[i, PAD : PAD + NB, 0:NB] = jnp.where(keep, dbuf[i].astype(F32), 0.0).astype(BF16)
-        pc = coupled(i)
-        turned = nt_dot(eye, pc.astype(BF16))
-        wts[i, 2 * PAD : 2 * PAD + NB, 0:NB] = jnp.where(keep, turned, 0.0).astype(BF16)
+        use_diagonal(i)
         if i + 1 < NE:
-            keep_next = lanes_nb < size_of(i + 1)
-            wts[i + 1, 0:NB, 0:NB] = jnp.where(keep_next, pc, 0.0).astype(BF16)
+            use_coupling(i)
 
     pl.semaphore_wait(barrier, len(friends))
 
+    def outer(k, src, dst, who):
+        return remote(src, dst, ext_send.at[k], ext_recv.at[k], who)
+
+    first, last = core * NE, core * NE + NE
     swap = remote(bands.at[:, theirs], raw.at[my_rows], gat_send.at[9], gat_recv.at[9], partner)
     swap.start()
-    pass_c = remote(csend, cprev, gat_send.at[10], gat_recv.at[10], right)
-    pass_c.start()
-
-    def slot(i):
-        return slice(PAD * i, PAD * (i + 1))
-
-    def halo(m, side):
-        v = buf.at[m % 2]
-        if side == 0:
-            src, dst, who = v.at[:, slot(1)], v.at[:, slot(NE + 1)], left
-        else:
-            src, dst, who = v.at[:, slot(NE)], v.at[:, slot(0)], right
-        return remote(src, dst, halo_send.at[m % 2, side], halo_recv.at[m % 2, side], who)
+    n_c, n_d = DEEP - 1, DEEP - 1
+    blocks = [
+        outer(0, sizes_hbm, sizes_left, right),
+        outer(1, pattern_hbm, pattern_left, right),
+        outer(2, hc.at[pl.ds(last - DEEP, DEEP)], cbuf.at[0:DEEP], right),
+        outer(3, hd.at[pl.ds(last - n_d, n_d)], dbuf.at[0:n_d], right),
+        outer(4, sizes_hbm, sizes_right, left),
+        outer(5, pattern_hbm, pattern_right, left),
+        outer(6, hc.at[pl.ds(first, n_c)], cbuf.at[DEEP + NE : DEEP + NE + n_c], left),
+        outer(7, hd.at[pl.ds(first, n_d)], dbuf.at[n_d + NE : n_d + NE + n_d], left),
+    ]
+    for copy in blocks:
+        copy.start()
 
     load_v.wait()
     swap.wait_recv()
+    vectors = [
+        outer(8, raw.at[:, COLS - EDGE : COLS], edges.at[0], right),
+        outer(9, raw.at[:, 0:EDGE], edges.at[1], left),
+    ]
+    for copy in vectors:
+        copy.start()
+
     lanes_pad = lax.broadcasted_iota(jnp.int32, (ROWS, PAD), 1)
 
-    def expand(i):
-        start = (NB * i) // 128 * 128
-        off = NB * i - start
-        x = raw[:, start : start + PAD].astype(F32)
+    def expand(i, ref, column):
+        start = column // 128 * 128
+        off = column - start
+        x = ref[:, start : start + PAD].astype(F32)
         if off:
             x = pltpu.roll(x, PAD - off, 1)
-        buf[0, :, slot(i + 1)] = jnp.where(lanes_pad < size_of(i), x, 0.0).astype(BF16)
-
-    expand(0)
-    halo(0, 0).start()
-    expand(NE - 1)
-    halo(0, 1).start()
-    for i in range(1, NE - 1):
-        expand(i)
-    pass_c.wait_recv()
-    wts[0, 0:NB, 0:NB] = jnp.where(lanes_nb < size_of(0), cprev[...].astype(F32), 0.0).astype(BF16)
+        buf[0, :, slot(i)] = jnp.where(lanes_pad < size_of(i), x, 0.0).astype(BF16)
+
+    for i in range(NE):
+        expand(i, raw, NB * i)
 
     def element(t, i):
-        now, then = t % 2, (t + 1) % 2
+        now, prior, targets = [
+            (0, None, [1]),
+            (1, 0, [0, 2]),
+            (0, 1, [1, 3]),
+            (3, 2, [2]),
+            (2, 3, [3]),
+            (3, 2, [2]),
+        ][t]
         acc = jnp.dot(
-            buf[now, :, PAD * i : PAD * (i + 3)], wts[i], preferred_element_type=F32
+            buf[now, :, slot(i - 1, 3)], wts[i + DEEP - 1], preferred_element_type=F32
         )
-        shifted = acc - CENTER * buf[now, :, slot(i + 1)].astype(F32)
+        shifted = acc - CENTER * buf[now, :, slot(i)].astype(F32)
         if t == 0:
             nxt = shifted * (1.0 / HALF)
         else:
-            nxt = shifted * (2.0 / HALF) - buf[then, :, slot(i + 1)].astype(F32)
-        buf[then, :, slot(i + 1)] = nxt.astype(BF16)
-
-    for t in range(DEGREE):
-        halo(t, 1).wait_recv()
-        if t >= 1:
-            halo(t - 1, 0).wait_send()
-        element(t, 0)
-        if t + 1 < DEGREE:
-            halo(t + 1, 0).start()
-        halo(t, 0).wait_recv()
-        if t >= 1:
-            halo(t - 1, 1).wait_send()
-        element(t, NE - 1)
-        if t + 1 < DEGREE:
-            halo(t + 1, 1).start()
-        for i in range(1, NE - 1):
-            element(t, i)
-
-    final = DEGREE % 2
+            nxt = shifted * (2.0 / HALF) - buf[prior, :, slot(i)].astype(F32)
+        nxt = nxt.astype(BF16)
+        for target in targets:
+            if target >= 2 and t < DEEP and not 0 <= i < NE:
+                continue
+            buf[target, :, slot(i)] = nxt
+
+    def inside(t0):
+        for k in range(DEEP):
+            for i in range(k + 1, NE - k - 1):
+                element(t0 + k, i)
+
+    def left_side(t0, k):
+        for i in range(k + 1 - DEEP, k + 1):
+            element(t0 + k, i)
+
+    def right_side(t0, k):
+        for i in range(NE - k - 1, NE + DEEP - k - 1):
+            element(t0 + k, i)
+
+    inside(0)
+    for copy in blocks:
+        copy.wait_recv()
+    use_coupling(NE - 1)
+    for i in range(1, DEEP):
+        use_coupling(-i)
+        use_coupling(NE + i - 1)
+        use_diagonal(-i)
+        use_diagonal(NE + i - 1)
+    use_coupling(-DEEP)
+    for copy in vectors:
+        copy.wait_recv()
+    for i in range(DEEP):
+        expand(i - DEEP, edges.at[0], EDGE - NB * (DEEP - i))
+        expand(NE + i, edges.at[1], NB * i)
+
+    def pass_on(k, source, target, n):
+        v, w = buf.at[source], buf.at[target]
+        return [
+            outer(k, v.at[:, slot(NE - n, n)], w.at[:, slot(-n, n)], right),
+            outer(k + 1, v.at[:, slot(0, n)], w.at[:, slot(NE, n)], left),
+        ]
+
+    second = pass_on(10, 0, 2, DEEP - 1)
+    third = pass_on(12, 1, 3, DEEP)
+    for k in range(DEEP):
+        left_side(0, k)
+        if k == 1:
+            second[1].start()
+        if k == 2:
+            third[1].start()
+        right_side(0, k)
+        if k == 1:
+            second[0].start()
+        if k == 2:
+            third[0].start()
+    inside(DEEP)
+    for copy in second + third:
+        copy.wait_recv()
+    for k in range(DEEP):
+        left_side(DEEP, k)
+        right_side(DEEP, k)
+
+    final = 2
     chunks = {}
     for i in range(NE):
         start = (NB * i) // 128
         off = NB * i - 128 * start
-        x = buf[final, :, slot(i + 1)].astype(F32)
+        x = buf[final, :, slot(i)].astype(F32)
         if off:
             x = pltpu.roll(x, off, 1)
         for k in range(2):
@@ -406,9 +484,8 @@
     for copy in sends:
         copy.wait_send()
     swap.wait_send()
-    pass_c.wait_send()
-    halo(DEGREE - 1, 0).wait_send()
-    halo(DEGREE - 1, 1).wait_send()
+    for copy in blocks + vectors + second + third:
+        copy.wait_send()
     keep_own.wait()
     give.wait()
 
@@ -424,13 +501,12 @@
         in_specs=[hbm] * 5,
         out_specs=hbm,
         scratch_shapes=[
-            pltpu.VMEM((NE, 3 * PAD, PAD), BF16),
-            pltpu.VMEM((2, ROWS, PAD * (NE + 2)), BF16),
-            pltpu.VMEM((NE, NB, NB), BF16),
-            pltpu.VMEM((NE, NB, NB), BF16),
-            pltpu.VMEM((NB, NB), BF16),
-            pltpu.VMEM((NB, NB), BF16),
+            pltpu.VMEM((NE + 2 * DEEP - 2, 3 * PAD, PAD), BF16),
+            pltpu.VMEM((4, ROWS, PAD * (NE + 2 * DEEP)), BF16),
+            pltpu.VMEM((NE + 2 * DEEP - 2, NB, NB), BF16),
+            pltpu.VMEM((NE + 2 * DEEP - 1, NB, NB), BF16),
             pltpu.VMEM((ROWS, COLS), BF16),
+            pltpu.VMEM((2, ROWS, EDGE), BF16),
             pltpu.VMEM((CHIPS, ROWS, COLS), BF16),
             pltpu.VMEM((2, ROWS, SIDE), F32),
             pltpu.VMEM((2, HALFROWS, SIDE), BF16),
@@ -444,11 +520,10 @@
             pltpu.VMEM((11, CHIPS, ROWS), F32),
             pltpu.VMEM((ROWS, BANDS), BF16),
             pltpu.VMEM((ROWS, COLS), BF16),
-            pltpu.SMEM((2 * NE,), jnp.int32),
-            pltpu.SMEM((2 * NE,), jnp.int32),
+            *[pltpu.SMEM((2 * NE,), jnp.int32)] * 6,
             dma((7,)),
-            dma((2, 2)),
-            dma((2, 2)),
+            dma((14,)),
+            dma((14,)),
             dma((12,)),
             dma((12,)),
             dma((27,)),

time: 82.1 us -> 73.9 us (0.900)
  Pallas kernels: 80.2 us -> 72 us
    pallas_call x1, Pallas kernels: 80.2 us -> 72 us  [shards(): pl.pallas_call(functools.partial(kernel, total_rows), out_shape=jax.Shape...]
where the time goes in v3:
time: 73.9 us; the launch traced here: 73.7 us
  Pallas kernels  72 us (97%)
  local copies, waits for them, and re-layouts  1.72 us (2%)
    pallas_call x1, Pallas kernels, shards(): pl.pallas_call(functools.partial(kernel, total_rows), out_shape=jax.Shape...  72 us
    unnamed x1, local copies, waits for them, and re-layouts  1.72 us

profile of v3, /device:TPU:1, one launch (start us, length us, event | category | flops | bytes accessed | tf_op | source)
XLA Modules:
  0.0 73.7 jit_solution(2276399404164462971)
XLA Ops:
  0.0 72.0 %filter_step.1 = bf16[64,2560]{1,0:T(8,128)(2,1)} custom-call(s32[16]{0:T(128)} %sizes_hbm.1, s32[16]{0:T(128)} %pattern_hbm.1, bf16[16,160,160]{2,1,0:T(8,128)(2,1)} %hd.1, bf16[16,160,160]{2,1,0:T(8,128)(2,1)} %hc.1, bf16[64,2560]{1,0:T(8,128)(2,1)} %bands.1), custom_call_target="tpu_custom_call" | custom-call | tf_op jit(solution)/shard_map/filter_step/pallas_call | solution.py:498
  72.0 1.7 %copy.7 = bf16[64,2560]{1,0:T(8,128)(2,1)} copy(bf16[64,2560]{1,0:T(8,128)(2,1)} %filter_step.1) | data formatting | bytes 655360

commit v4 on v3

v4 whole, which is shorter than its diff:
```python
import functools
import math

import jax
import jax.numpy as jnp
from jax import lax
from jax.experimental import pallas as pl
from jax.experimental.pallas import tpu as pltpu
from jax.sharding import PartitionSpec as P

MESH = pl.DeviceIdType.MESH
DEGREE = 6
CENTER = 0.4
HALF = 2.8
EPS = 1e-06
F32 = jnp.float32
BF16 = jnp.bfloat16

NB = 160
PAD = 256
NE = 8
ROWS = 128
HALFROWS = 64
COLS = NE * NB
DEEP = 3
EDGE = 512
ZL = 4
ZN = 16
XL = 2
NY = 4
CHIPS = 8
BANDS = ROWS * CHIPS
SIDE = ROWS * NY


def nt_dot(a, b):
    return lax.dot_general(a, b, (((1,), (1,)), ((), ())), preferred_element_type=F32)


def kernel(
    total_rows,
    sizes_hbm,
    pattern_hbm,
    hd,
    hc,
    bands,
    out_low,
    out_high,
    wts,
    buf,
    dbuf,
    cbuf,
    raw,
    edges,
    fall,
    strip,
    s1,
    r1,
    s2,
    r2,
    s3,
    r3,
    s4,
    sqs,
    sqr,
    wfull,
    obuf,
    sizes,
    pattern,
    sizes_out,
    pattern_out,
    local_sem,
    ext_send,
    ext_recv,
    gat_send,
    gat_recv,
    red_send,
    red_recv,
    sq_send,
    sq_recv,
):
    e = lax.axis_index("elem")
    b = lax.axis_index("band")
    ne = lax.axis_size("elem")
    core = b % 2
    other = 1 - core
    chip = b // 2
    xh = chip // NY
    y = chip % NY
    xl = e // ZN
    z = e % ZN
    zh = z // ZL
    zl = z % ZL

    def at(e_, b_):
        return (e_, b_)

    partner = at(e, chip * 2 + other)
    first = core == 0
    across_chip = at((e + jnp.where(first, ne - 1, 1)) % ne, chip * 2 + other)
    xpeer = at(e, ((1 - xh) * NY + y) * 2 + core)
    yup = at(e, (xh * NY + (y + 1) % NY) * 2 + core)
    ydn = at(e, (xh * NY + (y + NY - 1) % NY) * 2 + core)
    places = [((xl + j // ZL) % XL) * ZN + zh * ZL + (zl + j) % ZL for j in range(XL * ZL)]
    near = [at(p, b) for p in places[1:]]
    across = [at(p, xpeer[1]) for p in places]
    far = [at(xl * ZN + ((zh + j) % ZL) * ZL + zl, b) for j in range(1, ZL)]

    barrier = pltpu.get_barrier_semaphore()
    friends = [partner, across_chip, yup, ydn] + near + across + far
    for who in friends:
        pl.semaphore_signal(barrier, inc=1, device_id=who, device_id_type=MESH)

    def remote(src, dst, ss, rs, who):
        return pltpu.make_async_remote_copy(
            src_ref=src, dst_ref=dst, send_sem=ss, recv_sem=rs, device_id=who, device_id_type=MESH
        )

    def aligned(x, n):
        return pl.multiple_of(x, n)

    my_rows = pl.ds(aligned(core * HALFROWS, HALFROWS), HALFROWS)
    other_rows = pl.ds(aligned(other * HALFROWS, HALFROWS), HALFROWS)

    n_c, n_d = NE + DEEP, NE + DEEP - 1
    c_at, d_at = jnp.where(first, DEEP, 0), jnp.where(first, DEEP - 1, 0)
    load_c = pltpu.make_async_copy(
        hc.at[pl.ds(core * (NE - DEEP), n_c)], cbuf.at[pl.ds(c_at, n_c)], local_sem.at[0]
    )
    load_d = pltpu.make_async_copy(
        hd.at[pl.ds(core * (NE - DEEP + 1), n_d)], dbuf.at[pl.ds(d_at, n_d)], local_sem.at[1]
    )
    wide = COLS + EDGE
    base = aligned(core * EDGE, 128)
    mine = pl.ds(aligned(core * (COLS - EDGE), 128), wide)
    theirs = pl.ds(aligned(other * (COLS - EDGE), 128), wide)
    load_v = pltpu.make_async_copy(bands.at[:, mine], raw.at[my_rows], local_sem.at[2])
    load_s = pltpu.make_async_copy(sizes_hbm, sizes, local_sem.at[5])
    load_p = pltpu.make_async_copy(pattern_hbm, pattern, local_sem.at[6])
    for load in (load_s, load_p, load_c, load_d, load_v):
        load.start()

    pl.semaphore_wait(barrier, len(friends))

    def outer(k, src, dst, who):
        return remote(src, dst, ext_send.at[k], ext_recv.at[k], who)

    swap = remote(bands.at[:, theirs], raw.at[my_rows], gat_send.at[13], gat_recv.at[13], partner)
    swap.start()
    c_out = jnp.where(first, 0, 2 * NE - DEEP)
    d_out = jnp.where(first, 0, 2 * NE - DEEP + 1)
    c_in, d_in = jnp.where(first, DEEP + NE, 0), jnp.where(first, DEEP - 1 + NE, 0)
    blocks = [
        outer(0, sizes_hbm, sizes_out, across_chip),
        outer(1, pattern_hbm, pattern_out, across_chip),
        outer(2, hc.at[pl.ds(c_out, DEEP)], cbuf.at[pl.ds(c_in, DEEP)], across_chip),
        outer(3, hd.at[pl.ds(d_out, DEEP - 1)], dbuf.at[pl.ds(d_in, DEEP - 1)], across_chip),
    ]
    for copy in blocks:
        copy.start()

    wts[...] = jnp.zeros_like(wts)
    load_v.wait()
    swap.wait_recv()
    edge_out = pl.ds(aligned(core * COLS, 128), EDGE)
    vectors = outer(4, raw.at[:, edge_out], edges, across_chip)
    vectors.start()

    ICI, CHIP = 0, 1

    def on_side(side, j):
        return jnp.where(first, j, NE - 1 - j) if side == ICI else jnp.where(first, NE - 1 - j, j)

    def number(table, table_out, side, j):
        if side == ICI and j < 0:
            return table_out[jnp.where(first, 2 * NE + j, -1 - j)]
        if side == ICI:
            return table[jnp.where(first, j, 2 * NE - 1 - j)]
        return table[jnp.where(first, NE - 1 - j, NE + j)]

    lanes_nb = lax.broadcasted_iota(jnp.int32, (NB, NB), 1)
    eye = (lax.broadcasted_iota(jnp.int32, (NB, NB), 0) == lanes_nb).astype(BF16)

    def coupled(i, on):
        gate = jnp.full((NB, NB), on, jnp.int32) != 0
        return jnp.where(gate, cbuf[i + DEEP].astype(F32), 0.0)

    def put_weights(i, row, value, size):
        at_row = slice(row * PAD, row * PAD + NB)
        keep = lanes_nb < size
        wts[i + DEEP - 1, at_row, 0:NB] = jnp.where(keep, value, 0.0).astype(BF16)

    for load in (load_s, load_p, load_c, load_d):
        load.wait()
    own_size = [sizes[core * NE + i] for i in range(NE)]
    for i in range(NE):
        put_weights(i, 1, dbuf[i + DEEP - 1].astype(F32), own_size[i])
        if i + 1 < NE:
            pc = coupled(i, pattern[core * NE + i])
            put_weights(i, 2, nt_dot(eye, pc.astype(BF16)), own_size[i])
            put_weights(i + 1, 0, pc, own_size[i + 1])

    def side_weights(side):
        left_side = first if side == ICI else jnp.logical_not(first)
        count = number

        for j in range(-1, -DEEP, -1):
            i = on_side(side, j)
            size = count(sizes, sizes_out, side, j)
            put_weights(i, 1, dbuf[i + DEEP - 1].astype(F32), size)
        for j in range(0, -DEEP, -1):
            low = jnp.where(left_side, on_side(side, j - 1), on_side(side, j))
            on = jnp.where(
                left_side,
                count(pattern, pattern_out, side, j - 1),
                count(pattern, pattern_out, side, j),
            )
            pc = coupled(low, on)
            turned = nt_dot(eye, pc.astype(BF16))
            inner, outer_ = on_side(side, j), on_side(side, j - 1)
            size = count(sizes, sizes_out, side, j)
            value = jnp.where(left_side, pc, turned)
            put_weights_at(inner, jnp.where(left_side, 0, 2), value, size)
            if j > 1 - DEEP:
                size = count(sizes, sizes_out, side, j - 1)
                value = jnp.where(left_side, turned, pc)
                put_weights_at(outer_, jnp.where(left_side, 2, 0), value, size)

    def put_weights_at(i, row, value, size):
        keep = lanes_nb < size
        rows = pl.ds(aligned(row * PAD, PAD), NB)
        wts[i + DEEP - 1, rows, 0:NB] = jnp.where(keep, value, 0.0).astype(BF16)

    def slot(i, n=1):
        if isinstance(i, int):
            return slice(PAD * (i + DEEP), PAD * (i + DEEP + n))
        return pl.ds(aligned(PAD * (i + DEEP), PAD), PAD * n)

    lanes_pad = lax.broadcasted_iota(jnp.int32, (ROWS, PAD), 1)

    def expand(i, size, ref, column):
        off = column % 128
        x = ref[:, pl.ds(aligned(column - off, 128), PAD)].astype(F32)
        x = pltpu.roll(x, (PAD - off) % PAD, 1)
        buf[0, :, slot(i)] = jnp.where(lanes_pad < size, x, 0.0).astype(BF16)

    for i in range(NE):
        start = NB * i // 128 * 128
        x = raw[:, pl.ds(aligned(base + start, 128), PAD)].astype(F32)
        if NB * i > start:
            x = pltpu.roll(x, PAD - (NB * i - start), 1)
        buf[0, :, slot(i)] = jnp.where(lanes_pad < own_size[i], x, 0.0).astype(BF16)
    for j in range(-1, -DEEP - 1, -1):
        column = jnp.where(first, COLS + NB * (-1 - j), EDGE + NB * j)
        expand(on_side(CHIP, j), number(sizes, sizes_out, CHIP, j), raw, column)

    def element(t, i, own):
        now, prior, targets = [
            (0, None, [1]),
            (1, 0, [0, 2]),
            (0, 1, [1, 3]),
            (3, 2, [2]),
            (2, 3, [3]),
            (3, 2, [2]),
        ][t]
        acc = jnp.dot(
            buf[now, :, slot(i - 1, 3)], wts[i + DEEP - 1], preferred_element_type=F32
        )
        shifted = acc - CENTER * buf[now, :, slot(i)].astype(F32)
        if t == 0:
            nxt = shifted * (1.0 / HALF)
        else:
            nxt = shifted * (2.0 / HALF) - buf[prior, :, slot(i)].astype(F32)
        nxt = nxt.astype(BF16)
        for target in targets:
            if own or target < 2 or t >= DEEP:
                buf[target, :, slot(i)] = nxt

    def inside(t0):
        for k in range(DEEP):
            for i in range(k + 1, NE - k - 1):
                element(t0 + k, i, True)

    def side_steps(t0, side, k):
        for j in range(k + 1 - DEEP, k + 1):
            element(t0 + k, on_side(side, j), j >= 0)

    def pass_on(k, side, source, target, n):
        v, w = buf.at[source], buf.at[target]
        left_side = first if side == ICI else jnp.logical_not(first)
        src = slot(jnp.where(left_side, 0, NE - n), n)
        dst = slot(jnp.where(left_side, NE, -n), n)
        return outer(k, v.at[:, src], w.at[:, dst], across_chip if side == ICI else partner)

    second = [pass_on(5 + side, side, 0, 2, DEEP - 1) for side in (ICI, CHIP)]
    third = [pass_on(7 + side, side, 1, 3, DEEP) for side in (ICI, CHIP)]

    def first_steps(side):
        for k in range(DEEP):
            side_steps(0, side, k)
            if k == DEEP - 2:
                second[side].start()
        third[side].start()

    side_weights(CHIP)
    inside(0)
    first_steps(CHIP)
    for copy in blocks:
        copy.wait_recv()
    side_weights(ICI)
    vectors.wait_recv()
    for j in range(-1, -DEEP - 1, -1):
        column = jnp.where(first, EDGE + NB * j, NB * (-1 - j))
        expand(on_side(ICI, j), number(sizes, sizes_out, ICI, j), edges, column)
    first_steps(ICI)
    inside(DEEP)
    for side in (CHIP, ICI):
        second[side].wait_recv()
        third[side].wait_recv()
        for k in range(DEEP):
            side_steps(DEEP, side, k)

    final = 2
    chunks = {}
    for i in range(NE):
        start = (NB * i) // 128
        off = NB * i - 128 * start
        x = buf[final, :, slot(i)].astype(F32)
        if off:
            x = pltpu.roll(x, off, 1)
        for k in range(2):
            part = x[:, 128 * k : 128 * (k + 1)]
            at_chunk = start + k
            chunks[at_chunk] = chunks[at_chunk] + part if at_chunk in chunks else part
        done_to = COLS // 128 if i == NE - 1 else (NB * (i + 1)) // 128
        for c in sorted(chunks):
            if c < done_to:
                fall[core, chip, :, 128 * c : 128 * (c + 1)] = chunks.pop(c).astype(BF16)

    y_up, y_dn, y_far = (y + 1) % NY, (y + NY - 1) % NY, (y + 2) % NY
    peer_chip = (1 - xh) * NY + y
    side, far_side = xh * NY, (1 - xh) * NY
    low, high = slice(0, HALFROWS), slice(HALFROWS, ROWS)

    held = fall.at[core]

    def gather(k, g, rows, who):
        part = held.at[g] if rows is None else held.at[g, rows]
        copy = remote(part, part, gat_send.at[k], gat_recv.at[k], who)
        copy.start()
        sends.append(copy)
        return copy

    def share(k, g):
        copy = gather(14 + k, g, None, partner)
        shared.append(copy)

    sends, shared = [], []
    from_dn = [gather(1, chip, low, yup)]
    from_up = [gather(3, chip, high, ydn)]
    from_x = gather(0, chip, None, xpeer)
    from_dn.append(gather(2, chip, high, yup))
    from_up.append(gather(4, chip, low, ydn))
    share(0, chip)

    r128 = lax.broadcasted_iota(jnp.int32, (ROWS, ROWS), 0)
    c128 = lax.broadcasted_iota(jnp.int32, (ROWS, ROWS), 1)
    r8 = lax.broadcasted_iota(jnp.int32, (CHIPS, ROWS), 0)
    sqs[0] = jnp.zeros((CHIPS, ROWS), F32)

    def cols_of(y_):
        return pl.ds(pl.multiple_of(y_ * ROWS, ROWS), ROWS)

    def norms(g):
        there = held[g]
        square = nt_dot(there, there)
        diag = jnp.sum(jnp.where(r128 == c128, square, 0.0), axis=0, keepdims=True)
        sqs[0] = jnp.where(r8 == g, diag, sqs[0])

    def gram(part, g, y_):
        strip[part, :, cols_of(y_)] = nt_dot(held[g], held[side + y_])

    gram(0, chip, y)
    norms(chip)
    from_dn[0].wait_recv()
    on_up = gather(5, side + y_dn, low, yup)
    from_up[0].wait_recv()
    on_dn = gather(6, side + y_up, high, ydn)
    from_dn[1].wait_recv()
    share(1, side + y_dn)
    gram(0, chip, y_dn)
    norms(side + y_dn)
    from_up[1].wait_recv()
    share(2, side + y_up)
    gram(0, chip, y_up)
    norms(side + y_up)
    from_x.wait_recv()
    late_dn = [gather(7, peer_chip, low, yup)]
    late_up = [gather(9, peer_chip, high, ydn)]
    late_dn.append(gather(8, peer_chip, high, yup))
    late_up.append(gather(10, peer_chip, low, ydn))
    norms(peer_chip)
    gram(1, peer_chip, y)
    gram(1, peer_chip, y_dn)
    gram(1, peer_chip, y_up)
    on_up.wait_recv()
    on_dn.wait_recv()
    gram(0, chip, y_far)
    gram(1, peer_chip, y_far)
    norms(side + y_far)

    def stage(k, src, dst, who):
        return remote(src, dst, red_send.at[k], red_recv.at[k], who)

    def squares(k, s, who):
        return remote(sqs.at[s], sqr.at[k], sq_send.at[k], sq_recv.at[k], who)

    s1[...] = strip[:, other_rows, :].astype(BF16)
    copies = [stage(0, s1, r1, partner), squares(0, 0, partner)]
    for copy in copies:
        copy.start()
    for copy in copies:
        copy.wait_recv()
    half = strip[:, my_rows, :] + r1[...].astype(F32)
    strip[:, my_rows, :] = half
    s2[...] = half.astype(BF16)
    sqs[1] = sqs[0] + sqr[0]
    sends += copies
    share(3, side + y_far)
    share(4, peer_chip)

    quarter = HALFROWS // XL
    copies = []
    for j in range(1, XL * ZL):
        xl_, zl_ = (xl + j // ZL) % XL, (zl + j) % ZL
        rows = pl.ds(pl.multiple_of(xl_ * quarter, quarter), quarter)
        copies.append(stage(j, s2.at[:, rows, cols_of(zl_)], r2.at[j - 1], near[j - 1]))
        copies.append(squares(j, 1, near[j - 1]))
    for copy in copies:
        copy.start()
    row0 = pl.multiple_of(core * HALFROWS + xl * quarter, quarter)
    piece_rows = pl.ds(row0, quarter)
    total = strip[:, piece_rows, cols_of(zl)]
    sq = sqs[1]
    for copy in copies:
        copy.wait_recv()
    for j in range(1, XL * ZL):
        total = total + r2[j - 1].astype(F32)
        sq = sq + sqr[j]
    s3[...] = total.astype(BF16)
    sqs[2] = sq
    sends += copies

    copies = []
    for j in range(1, ZL):
        copies.append(stage(7 + j, s3, r3.at[j - 1], far[j - 1]))
        copies.append(squares(7 + j, 2, far[j - 1]))
    for copy in copies:
        copy.start()
    late_dn[0].wait_recv()
    late_on_up = gather(11, far_side + y_dn, low, yup)
    late_up[0].wait_recv()
    late_on_dn = gather(12, far_side + y_up, high, ydn)
    late_dn[1].wait_recv()
    share(5, far_side + y_dn)
    late_up[1].wait_recv()
    share(6, far_side + y_up)
    for copy in copies:
        copy.wait_recv()
    for j in range(1, ZL):
        total = total + r3[j - 1].astype(F32)
        sq = sq + sqr[7 + j]
    sends += copies

    scale = lax.rsqrt(sq + EPS)
    ri = lax.broadcasted_iota(jnp.int32, (quarter, ROWS), 0) + row0
    ci = lax.broadcasted_iota(jnp.int32, (quarter, ROWS), 1)
    same = ri == ci
    g = side + zl
    scale_row = jnp.sum(jnp.where(r8 == g, scale, 0.0), axis=0, keepdims=True)
    sq_row = jnp.sum(jnp.where(r8 == g, sq, 0.0), axis=0, keepdims=True)
    for part in range(2):
        of = chip if part == 0 else peer_chip
        lanes = jnp.sum(jnp.where(r8 == of, scale, 0.0), axis=0, keepdims=True)
        row_scale = jnp.sum(jnp.where(same, lanes, 0.0), axis=1, keepdims=True)
        value = total[part]
        ident = jnp.zeros_like(value)
        if part == 0:
            unit = jnp.logical_and(same, jnp.full(same.shape, zl - y, jnp.int32) == 0)
            value = jnp.where(unit, sq_row, value)
            ident = jnp.where(unit, 1.5, 0.0)
        normed = row_scale * value * scale_row
        w = math.sqrt(total_rows) * scale_row * (ident - 0.5 * normed)
        s4[part] = w.astype(BF16)

    g_cols = pl.ds(pl.multiple_of(g * ROWS, ROWS), ROWS)
    place = wfull.at[pl.ds(pl.multiple_of(xl * quarter, quarter), quarter), g_cols]
    put = pltpu.make_async_copy(s4.at[0], place, local_sem.at[4])
    put.start()
    copies = [stage(10 + j, s4.at[0], place, near[j - 1]) for j in range(1, XL * ZL)]
    copies += [stage(18 + j, s4.at[1], place, across[j]) for j in range(XL * ZL)]
    for copy in copies:
        copy.start()
    late_on_up.wait_recv()
    late_on_dn.wait_recv()
    share(7, far_side + y_far)
    for copy in shared:
        copy.wait_recv()
    for copy in copies:
        copy.wait_recv()
    put.wait()
    sends += copies

    writes = []
    for h in range(2):
        whole = fall.at[h].reshape(BANDS, COLS)
        for k in range(COLS // PAD):
            obuf[h, :, PAD * k : PAD * (k + 1)] = jnp.dot(
                wfull[...], whole[:, PAD * k : PAD * (k + 1)], preferred_element_type=F32
            ).astype(BF16)
        write = pltpu.make_async_copy(obuf.at[h], (out_low, out_high)[h], local_sem.at[3 + 4 * h])
        write.start()
        writes.append(write)
    for copy in sends + blocks + [vectors, swap] + second + third:
        copy.wait_send()
    for write in writes:
        write.wait()


def shards(basis_sizes, coupling_pattern, h_diag, h_couple, bands):
    total_rows = h_diag.shape[0] * lax.axis_size("elem") * h_diag.shape[1]
    hbm = pl.BlockSpec(memory_space=pltpu.HBM)
    dma = pltpu.SemaphoreType.DMA
    quarter = HALFROWS // XL
    halves = pl.pallas_call(
        functools.partial(kernel, total_rows),
        out_shape=[jax.ShapeDtypeStruct((HALFROWS, COLS), BF16)] * 2,
        in_specs=[hbm] * 5,
        out_specs=[hbm, hbm],
        scratch_shapes=[
            pltpu.VMEM((NE + 2 * DEEP - 2, 3 * PAD, PAD), BF16),
            pltpu.VMEM((4, ROWS, PAD * (NE + 2 * DEEP)), BF16),
            pltpu.VMEM((NE + 2 * DEEP - 2, NB, NB), BF16),
            pltpu.VMEM((NE + 2 * DEEP, NB, NB), BF16),
            pltpu.VMEM((ROWS, COLS + EDGE), BF16),
            pltpu.VMEM((ROWS, EDGE), BF16),
            pltpu.VMEM((2, CHIPS, ROWS, COLS), BF16),
            pltpu.VMEM((2, ROWS, SIDE), F32),
            pltpu.VMEM((2, HALFROWS, SIDE), BF16),
            pltpu.VMEM((2, HALFROWS, SIDE), BF16),
            pltpu.VMEM((2, HALFROWS, SIDE), BF16),
            pltpu.VMEM((XL * ZL - 1, 2, quarter, ROWS), BF16),
            pltpu.VMEM((2, quarter, ROWS), BF16),
            pltpu.VMEM((ZL - 1, 2, quarter, ROWS), BF16),
            pltpu.VMEM((2, quarter, ROWS), BF16),
            pltpu.VMEM((3, CHIPS, ROWS), F32),
            pltpu.VMEM((11, CHIPS, ROWS), F32),
            pltpu.VMEM((HALFROWS, BANDS), BF16),
            pltpu.VMEM((2, HALFROWS, COLS), BF16),
            *[pltpu.SMEM((2 * NE,), jnp.int32)] * 4,
            dma((8,)),
            dma((9,)),
            dma((9,)),
            dma((22,)),
            dma((22,)),
            dma((26,)),
            dma((26,)),
            dma((11,)),
            dma((11,)),
        ],
        compiler_params=pltpu.CompilerParams(
            collective_id=0, has_side_effects=True, vmem_limit_bytes=67043328
        ),
        name="filter_step",
    )(basis_sizes, coupling_pattern, h_diag, h_couple, bands)
    return jnp.concatenate(halves, axis=1)


def solution(mesh):
    in_specs = (
        P("elem"),
        P("elem"),
        P("elem", None, None),
        P("elem", None, None),
        P("band", "elem"),
    )
    out_specs = P("band", "elem")
    return jax.shard_map(shards, mesh=mesh, in_specs=in_specs, out_specs=out_specs, check_vma=False)
```

time: 73.9 us -> 71.6 us (0.969)
  Pallas kernels: 72 us -> 69.7 us
  other arithmetic: 0 us -> 1.74 us
  local copies, waits for them, and re-layouts: 1.72 us -> 0 us
    pallas_call x1, Pallas kernels: 72 us -> 69.7 us  [shards(): pl.pallas_call(functools.partial(kernel, total_rows), out_shape=[jax.Shap...]
    concatenate x0 -> x1, other arithmetic: none -> 1.74 us  [shards(): return jnp.concatenate(halves, axis=1)]
    unnamed x1 -> x0, local copies, waits for them, and re-layouts: 1.72 us -> none
where the time goes in v4:
time: 71.6 us; the launch traced here: 71.5 us
  Pallas kernels  69.7 us (97%)
  other arithmetic  1.74 us (2%)
    pallas_call x1, Pallas kernels, shards(): pl.pallas_call(functools.partial(kernel, total_rows), out_shape=[jax.Shap...  69.7 us
    concatenate x1, other arithmetic, shards(): return jnp.concatenate(halves, axis=1)  1.74 us

profile of v4, /device:TPU:1, one launch (start us, length us, event | category | flops | bytes accessed | tf_op | source)
XLA Modules:
  0.0 71.5 jit_solution(17248272063728073710)
XLA Ops:
  0.0 69.7 %filter_step.1 = (bf16[64,1280]{1,0:T(8,128)(2,1)}, bf16[64,1280]{1,0:T(8,128)(2,1)}) custom-call(s32[16]{0:T(128)} %sizes_hbm.1, s32[16]{0:T(128)} %pattern_hbm.1, bf16[16,160,160]{2,1,0:T(8,128)(2,1)} %hd.1, bf16[16,160,160]{2,1,0:T(8,128)(2,1)} %hc.1, bf16[64,2560]{1,0:T(8,128)(2,1)} %bands.1), custom_call_target="tpu_custom_call" | custom-call | tf_op jit(solution)/shard_map/filter_step/pallas_call | solution.py:535
  69.7 1.7 %pad_maximum_fusion = bf16[64,2560]{1,0:T(8,128)(2,1)} fusion(bf16[64,1280]{1,0:T(8,128)(2,1)} %get-tuple-element.8, bf16[64,1280]{1,0:T(8,128)(2,1)} %get-tuple-element.7), kind=kLoop, calls=%fused_computation | loop fusion | flops 655360 | bytes 655360 | tf_op jit(solution)/shard_map/concatenate | solution.py:576

commit v5 on v4

--- a/solution.py
+++ b/solution.py
@@ -30,7 +30,6 @@
 NY = 4
 CHIPS = 8
 BANDS = ROWS * CHIPS
-SIDE = ROWS * NY
 
 
 def nt_dot(a, b):
@@ -69,6 +68,9 @@
     pattern,
     sizes_out,
     pattern_out,
+    round1,
+    round2,
+    round3,
     local_sem,
     ext_send,
     ext_recv,
@@ -107,9 +109,16 @@
     far = [at(xl * ZN + ((zh + j) % ZL) * ZL + zl, b) for j in range(1, ZL)]
 
     barrier = pltpu.get_barrier_semaphore()
-    friends = [partner, across_chip, yup, ydn] + near + across + far
-    for who in friends:
-        pl.semaphore_signal(barrier, inc=1, device_id=who, device_id_type=MESH)
+    zs = [at(xl * ZN + (z + d) % ZN, b) for d in (1, ZN - 1, 2, ZN - 2)]
+    links = zs + [xpeer, at((1 - xl) * ZN + z, b), yup, ydn]
+    friends = [partner, across_chip] + links
+    yfar = at(e, (xh * NY + (y + 2) % NY) * 2 + core)
+
+    def tell(sem, whom):
+        for who in whom:
+            pl.semaphore_signal(sem, inc=1, device_id=who, device_id_type=MESH)
+
+    tell(barrier, friends)
 
     def remote(src, dst, ss, rs, who):
         return pltpu.make_async_remote_copy(
@@ -142,6 +151,8 @@
 
     pl.semaphore_wait(barrier, len(friends))
 
+    tell(round1, links)
+
     def outer(k, src, dst, who):
         return remote(src, dst, ext_send.at[k], ext_recv.at[k], who)
 
@@ -165,6 +176,9 @@
     edge_out = pl.ds(aligned(core * COLS, 128), EDGE)
     vectors = outer(4, raw.at[:, edge_out], edges, across_chip)
     vectors.start()
+
+    pl.semaphore_wait(round1, len(links))
+    tell(round2, links + [far[0], far[ZL - 2]])
 
     ICI, CHIP = 0, 1
 
@@ -283,17 +297,17 @@
 
     def side_steps(t0, side, k):
         for j in range(k + 1 - DEEP, k + 1):
-            element(t0 + k, on_side(side, j), j >= 0)
-
-    def pass_on(k, side, source, target, n):
+            element(t0 + k, on_side(side, j), j >= 0 or k == DEEP - 2)
+
+    def pass_on(k, side, source, target, skip, n):
         v, w = buf.at[source], buf.at[target]
         left_side = first if side == ICI else jnp.logical_not(first)
-        src = slot(jnp.where(left_side, 0, NE - n), n)
-        dst = slot(jnp.where(left_side, NE, -n), n)
+        src = slot(jnp.where(left_side, skip, NE - n - skip), n)
+        dst = slot(jnp.where(left_side, NE + skip, -n - skip), n)
         return outer(k, v.at[:, src], w.at[:, dst], across_chip if side == ICI else partner)
 
-    second = [pass_on(5 + side, side, 0, 2, DEEP - 1) for side in (ICI, CHIP)]
-    third = [pass_on(7 + side, side, 1, 3, DEEP) for side in (ICI, CHIP)]
+    second = [pass_on(5 + side, side, 0, 2, DEEP - 2, 1) for side in (ICI, CHIP)]
+    third = [pass_on(7 + side, side, 1, 3, 0, DEEP) for side in (ICI, CHIP)]
 
     def first_steps(side):
         for k in range(DEEP):
@@ -305,6 +319,8 @@
     side_weights(CHIP)
     inside(0)
     first_steps(CHIP)
+    pl.semaphore_wait(round2, len(links) + 2)
+    tell(round3, links)
     for copy in blocks:
         copy.wait_recv()
     side_weights(ICI)
@@ -319,6 +335,8 @@
         third[side].wait_recv()
         for k in range(DEEP):
             side_steps(DEEP, side, k)
+
+    pl.semaphore_wait(round3, len(links))
 
     final = 2
     chunks = {}
@@ -365,98 +383,119 @@
 
     r128 = lax.broadcasted_iota(jnp.int32, (ROWS, ROWS), 0)
     c128 = lax.broadcasted_iota(jnp.int32, (ROWS, ROWS), 1)
-    r8 = lax.broadcasted_iota(jnp.int32, (CHIPS, ROWS), 0)
-    sqs[0] = jnp.zeros((CHIPS, ROWS), F32)
-
-    def cols_of(y_):
-        return pl.ds(pl.multiple_of(y_ * ROWS, ROWS), ROWS)
-
-    def norms(g):
-        there = held[g]
-        square = nt_dot(there, there)
-        diag = jnp.sum(jnp.where(r128 == c128, square, 0.0), axis=0, keepdims=True)
-        sqs[0] = jnp.where(r8 == g, diag, sqs[0])
-
-    def gram(part, g, y_):
-        strip[part, :, cols_of(y_)] = nt_dot(held[g], held[side + y_])
-
-    gram(0, chip, y)
-    norms(chip)
+
+    def gram(part, g, o):
+        strip[o, part] = nt_dot(held[g], held[side + (y + o) % NY])
+
+    def squares(k, s, who):
+        copy = remote(sqs.at[s], sqr.at[k], sq_send.at[k], sq_recv.at[k], who)
+        copy.start()
+        sends.append(copy)
+        return copy
+
+    def stage(k, src, dst, who):
+        return remote(src, dst, red_send.at[k], red_recv.at[k], who)
+
+    quarter = HALFROWS // XL
+    row0 = pl.multiple_of(core * HALFROWS + xl * quarter, quarter)
+    piece_rows = pl.ds(row0, quarter)
+
+    def over_cores(offsets):
+        copies = []
+        for o in offsets:
+            s1[o] = strip[o, :, other_rows, :].astype(BF16)
+            copies.append(stage(o, s1.at[o], r1.at[o], partner))
+            copies[-1].start()
+        sends.extend(copies)
+        return copies
+
+    def to_owner(o, dx):
+        col = (y + o) % NY
+        j = dx * ZL + (col + ZL - zl) % ZL
+        xl_ = (xl + dx) % XL
+        rows = pl.ds(pl.multiple_of(xl_ * quarter, quarter), quarter)
+        who = at(xl_ * ZN + zh * ZL + col, b)
+        copy = remote(
+            s2.at[o, :, rows], r2.at[j - 1], red_send.at[j + 4], red_recv.at[j + 4], who
+        )
+        return copy, col != zl
+
+    def to_owners(offsets, copies):
+        for o, copy in zip(offsets, copies):
+            copy.wait_recv()
+            half = strip[o, :, my_rows, :] + r1[o].astype(F32)
+            strip[o, :, my_rows, :] = half
+            s2[o] = half.astype(BF16)
+            crossing, _ = to_owner(o, 1)
+            crossing.start()
+            along, away = to_owner(o, 0)
+
+            @pl.when(away)
+            def _():
+                along.start()
+
+    gram(0, chip, 0)
+    norm = jnp.sum(jnp.where(r128 == c128, strip[0, 0], 0.0), axis=0, keepdims=True)
+    sqs[0] = jnp.broadcast_to(norm, (CHIPS, ROWS))
+    of_core = squares(0, 0, partner)
     from_dn[0].wait_recv()
     on_up = gather(5, side + y_dn, low, yup)
     from_up[0].wait_recv()
     on_dn = gather(6, side + y_up, high, ydn)
+    of_core.wait_recv()
+    sqs[1] = sqs[0] + sqr[0]
+    of_near = [squares(j, 1, near[j - 1]) for j in range(1, XL * ZL)]
     from_dn[1].wait_recv()
-    share(1, side + y_dn)
-    gram(0, chip, y_dn)
-    norms(side + y_dn)
+    gram(0, chip, 3)
     from_up[1].wait_recv()
-    share(2, side + y_up)
-    gram(0, chip, y_up)
-    norms(side + y_up)
+    gram(0, chip, 1)
     from_x.wait_recv()
     late_dn = [gather(7, peer_chip, low, yup)]
     late_up = [gather(9, peer_chip, high, ydn)]
     late_dn.append(gather(8, peer_chip, high, yup))
     late_up.append(gather(10, peer_chip, low, ydn))
-    norms(peer_chip)
-    gram(1, peer_chip, y)
-    gram(1, peer_chip, y_dn)
-    gram(1, peer_chip, y_up)
+    early, last = (0, 3, 1), (2,)
+    for o in early:
+        gram(1, peer_chip, o)
+    first_sums = over_cores(early)
+    to_owners(early, first_sums)
+    for copy in of_near:
+        copy.wait_recv()
+    norm = sqs[1]
+    for j in range(1, XL * ZL):
+        norm = norm + sqr[j]
+    sqs[2] = norm
+    of_far = [squares(7 + j, 2, far[j - 1]) for j in range(1, ZL)]
     on_up.wait_recv()
     on_dn.wait_recv()
-    gram(0, chip, y_far)
-    gram(1, peer_chip, y_far)
-    norms(side + y_far)
-
-    def stage(k, src, dst, who):
-        return remote(src, dst, red_send.at[k], red_recv.at[k], who)
-
-    def squares(k, s, who):
-        return remote(sqs.at[s], sqr.at[k], sq_send.at[k], sq_recv.at[k], who)
-
-    s1[...] = strip[:, other_rows, :].astype(BF16)
-    copies = [stage(0, s1, r1, partner), squares(0, 0, partner)]
+    gram(0, chip, 2)
+    gram(1, peer_chip, 2)
+    last_sums = over_cores(last)
+    to_owners(last, last_sums)
+    share(1, side + y_dn)
+    share(2, side + y_up)
+    share(3, side + y_far)
+    share(4, peer_chip)
+
+    copies = [stage(4 + j, r2.at[j - 1], r2.at[j - 1], near[j - 1]) for j in range(1, XL * ZL)]
+    for copy in copies:
+        copy.wait_recv()
+    total = strip[(zl + NY - y) % NY, :, piece_rows, :]
+    for j in range(1, XL * ZL):
+        total = total + r2[j - 1].astype(F32)
+    s3[...] = total.astype(BF16)
+    copies = [stage(11 + j, s3, r3.at[j - 1], far[j - 1]) for j in range(1, ZL)]
     for copy in copies:
         copy.start()
-    for copy in copies:
-        copy.wait_recv()
-    half = strip[:, my_rows, :] + r1[...].astype(F32)
-    strip[:, my_rows, :] = half
-    s2[...] = half.astype(BF16)
-    sqs[1] = sqs[0] + sqr[0]
-    sends += copies
-    share(3, side + y_far)
-    share(4, peer_chip)
-
-    quarter = HALFROWS // XL
-    copies = []
-    for j in range(1, XL * ZL):
-        xl_, zl_ = (xl + j // ZL) % XL, (zl + j) % ZL
-        rows = pl.ds(pl.multiple_of(xl_ * quarter, quarter), quarter)
-        copies.append(stage(j, s2.at[:, rows, cols_of(zl_)], r2.at[j - 1], near[j - 1]))
-        copies.append(squares(j, 1, near[j - 1]))
-    for copy in copies:
-        copy.start()
-    row0 = pl.multiple_of(core * HALFROWS + xl * quarter, quarter)
-    piece_rows = pl.ds(row0, quarter)
-    total = strip[:, piece_rows, cols_of(zl)]
-    sq = sqs[1]
-    for copy in copies:
-        copy.wait_recv()
-    for j in range(1, XL * ZL):
-        total = total + r2[j - 1].astype(F32)
-        sq = sq + sqr[j]
-    s3[...] = total.astype(BF16)
-    sqs[2] = sq
-    sends += copies
-
-    copies = []
+    sends.extend(copies)
+
+    for copy in of_far:
+        copy.wait_recv()
+    norm = sqs[2]
     for j in range(1, ZL):
-        copies.append(stage(7 + j, s3, r3.at[j - 1], far[j - 1]))
-        copies.append(squares(7 + j, 2, far[j - 1]))
-    for copy in copies:
-        copy.start()
+        norm = norm + sqr[7 + j]
+    sqs[3] = norm
+    norms = [squares(11 + k, 3, who) for k, who in enumerate((yup, ydn, yfar, xpeer))]
     late_dn[0].wait_recv()
     late_on_up = gather(11, far_side + y_dn, low, yup)
     late_up[0].wait_recv()
@@ -465,23 +504,25 @@
     share(5, far_side + y_dn)
     late_up[1].wait_recv()
     share(6, far_side + y_up)
+    for copy in norms:
+        copy.wait_recv()
     for copy in copies:
         copy.wait_recv()
     for j in range(1, ZL):
         total = total + r3[j - 1].astype(F32)
-        sq = sq + sqr[7 + j]
-    sends += copies
-
-    scale = lax.rsqrt(sq + EPS)
+
     ri = lax.broadcasted_iota(jnp.int32, (quarter, ROWS), 0) + row0
     ci = lax.broadcasted_iota(jnp.int32, (quarter, ROWS), 1)
     same = ri == ci
     g = side + zl
-    scale_row = jnp.sum(jnp.where(r8 == g, scale, 0.0), axis=0, keepdims=True)
-    sq_row = jnp.sum(jnp.where(r8 == g, sq, 0.0), axis=0, keepdims=True)
+    by_offset = [sqs[3, 0:1], sqr[12, 0:1], sqr[13, 0:1], sqr[11, 0:1]]
+    sq_row = by_offset[0]
+    for o in range(1, NY):
+        here = jnp.full((1, ROWS), (zl + NY - y) % NY, jnp.int32) == o
+        sq_row = jnp.where(here, by_offset[o], sq_row)
+    scale_row = lax.rsqrt(sq_row + EPS)
     for part in range(2):
-        of = chip if part == 0 else peer_chip
-        lanes = jnp.sum(jnp.where(r8 == of, scale, 0.0), axis=0, keepdims=True)
+        lanes = lax.rsqrt((sqs[3, 0:1] if part == 0 else sqr[14, 0:1]) + EPS)
         row_scale = jnp.sum(jnp.where(same, lanes, 0.0), axis=1, keepdims=True)
         value = total[part]
         ident = jnp.zeros_like(value)
@@ -497,8 +538,8 @@
     place = wfull.at[pl.ds(pl.multiple_of(xl * quarter, quarter), quarter), g_cols]
     put = pltpu.make_async_copy(s4.at[0], place, local_sem.at[4])
     put.start()
-    copies = [stage(10 + j, s4.at[0], place, near[j - 1]) for j in range(1, XL * ZL)]
-    copies += [stage(18 + j, s4.at[1], place, across[j]) for j in range(XL * ZL)]
+    copies = [stage(14 + j, s4.at[0], place, near[j - 1]) for j in range(1, XL * ZL)]
+    copies += [stage(22 + j, s4.at[1], place, across[j]) for j in range(XL * ZL)]
     for copy in copies:
         copy.start()
     late_on_up.wait_recv()
@@ -521,6 +562,15 @@
         write = pltpu.make_async_copy(obuf.at[h], (out_low, out_high)[h], local_sem.at[3 + 4 * h])
         write.start()
         writes.append(write)
+    for o in range(NY):
+        crossing, _ = to_owner(o, 1)
+        crossing.wait_send()
+        along, away = to_owner(o, 0)
+
+        @pl.when(away)
+        def _():
+            along.wait_send()
+
     for copy in sends + blocks + [vectors, swap] + second + third:
         copy.wait_send()
     for write in writes:
@@ -545,28 +595,29 @@
             pltpu.VMEM((ROWS, COLS + EDGE), BF16),
             pltpu.VMEM((ROWS, EDGE), BF16),
             pltpu.VMEM((2, CHIPS, ROWS, COLS), BF16),
-            pltpu.VMEM((2, ROWS, SIDE), F32),
-            pltpu.VMEM((2, HALFROWS, SIDE), BF16),
-            pltpu.VMEM((2, HALFROWS, SIDE), BF16),
-            pltpu.VMEM((2, HALFROWS, SIDE), BF16),
+            pltpu.VMEM((NY, 2, ROWS, ROWS), F32),
+            pltpu.VMEM((NY, 2, HALFROWS, ROWS), BF16),
+            pltpu.VMEM((NY, 2, HALFROWS, ROWS), BF16),
+            pltpu.VMEM((NY, 2, HALFROWS, ROWS), BF16),
             pltpu.VMEM((XL * ZL - 1, 2, quarter, ROWS), BF16),
             pltpu.VMEM((2, quarter, ROWS), BF16),
             pltpu.VMEM((ZL - 1, 2, quarter, ROWS), BF16),
             pltpu.VMEM((2, quarter, ROWS), BF16),
-            pltpu.VMEM((3, CHIPS, ROWS), F32),
-            pltpu.VMEM((11, CHIPS, ROWS), F32),
+            pltpu.VMEM((4, CHIPS, ROWS), F32),
+            pltpu.VMEM((15, CHIPS, ROWS), F32),
             pltpu.VMEM((HALFROWS, BANDS), BF16),
             pltpu.VMEM((2, HALFROWS, COLS), BF16),
             *[pltpu.SMEM((2 * NE,), jnp.int32)] * 4,
+            *[pltpu.SemaphoreType.REGULAR] * 3,
             dma((8,)),
             dma((9,)),
             dma((9,)),
             dma((22,)),
             dma((22,)),
-            dma((26,)),
-            dma((26,)),
-            dma((11,)),
-            dma((11,)),
+            dma((30,)),
+            dma((30,)),
+            dma((15,)),
+            dma((15,)),
         ],
         compiler_params=pltpu.CompilerParams(
             collective_id=0, has_side_effects=True, vmem_limit_bytes=67043328

time: 71.6 us -> 65.2 us (0.911)
  Pallas kernels: 69.7 us -> 63.3 us
    pallas_call x1, Pallas kernels: 69.7 us -> 63.3 us  [shards(): pl.pallas_call(functools.partial(kernel, total_rows), out_shape=[jax.Shap...]
where the time goes in v5:
time: 65.2 us; the launch traced here: 65 us
  Pallas kernels  63.3 us (97%)
  other arithmetic  1.74 us (3%)
    pallas_call x1, Pallas kernels, shards(): pl.pallas_call(functools.partial(kernel, total_rows), out_shape=[jax.Shap...  63.3 us
    concatenate x1, other arithmetic, shards(): return jnp.concatenate(halves, axis=1)  1.74 us

profile of v5, /device:TPU:1, one launch (start us, length us, event | category | flops | bytes accessed | tf_op | source)
XLA Modules:
  0.0 65.0 jit_solution(10449042693225346911)
XLA Ops:
  0.0 63.3 %filter_step.1 = (bf16[64,1280]{1,0:T(8,128)(2,1)}, bf16[64,1280]{1,0:T(8,128)(2,1)}) custom-call(s32[16]{0:T(128)} %sizes_hbm.1, s32[16]{0:T(128)} %pattern_hbm.1, bf16[16,160,160]{2,1,0:T(8,128)(2,1)} %hd.1, bf16[16,160,160]{2,1,0:T(8,128)(2,1)} %hc.1, bf16[64,2560]{1,0:T(8,128)(2,1)} %bands.1), custom_call_target="tpu_custom_call" | custom-call | tf_op jit(solution)/shard_map/filter_step/pallas_call | solution.py:585
  63.3 1.7 %pad_maximum_fusion = bf16[64,2560]{1,0:T(8,128)(2,1)} fusion(bf16[64,1280]{1,0:T(8,128)(2,1)} %get-tuple-element.8, bf16[64,1280]{1,0:T(8,128)(2,1)} %get-tuple-element.7), kind=kLoop, calls=%fused_computation | loop fusion | flops 655360 | bytes 655360 | tf_op jit(solution)/shard_map/concatenate | solution.py:627

commit v6 on v5

--- a/solution.py
+++ b/solution.py
@@ -24,6 +24,7 @@
 COLS = NE * NB
 DEEP = 3
 EDGE = 512
+REST = NB - 128
 ZL = 4
 ZN = 16
 XL = 2
@@ -51,6 +52,8 @@
     cbuf,
     raw,
     edges,
+    tails,
+    packed,
     fall,
     strip,
     s1,
@@ -158,17 +161,28 @@
 
     swap = remote(bands.at[:, theirs], raw.at[my_rows], gat_send.at[13], gat_recv.at[13], partner)
     swap.start()
+    head, n_e = slice(0, 128), DEEP - 1
     c_out = jnp.where(first, 0, 2 * NE - DEEP)
     d_out = jnp.where(first, 0, 2 * NE - DEEP + 1)
     c_in, d_in = jnp.where(first, DEEP + NE, 0), jnp.where(first, DEEP - 1 + NE, 0)
     blocks = [
         outer(0, sizes_hbm, sizes_out, across_chip),
         outer(1, pattern_hbm, pattern_out, across_chip),
-        outer(2, hc.at[pl.ds(c_out, DEEP)], cbuf.at[pl.ds(c_in, DEEP)], across_chip),
-        outer(3, hd.at[pl.ds(d_out, DEEP - 1)], dbuf.at[pl.ds(d_in, DEEP - 1)], across_chip),
+        outer(2, hc.at[pl.ds(c_out, DEEP), :, head], cbuf.at[pl.ds(c_in, DEEP), :, head], across_chip),
+        outer(3, hd.at[pl.ds(d_out, n_e), :, head], dbuf.at[pl.ds(d_in, n_e), :, head], across_chip),
     ]
     for copy in blocks:
         copy.start()
+    for load in (load_s, load_p, load_c, load_d):
+        load.wait()
+    c_from = jnp.where(first, DEEP, NE)
+    d_from = jnp.where(first, DEEP - 1, NE)
+    for k in range(DEEP):
+        tails[0, :, REST * k : REST * (k + 1)] = cbuf[c_from + k, :, 128:NB]
+    for k in range(n_e):
+        tails[0, REST * k : REST * (k + 1), REST * DEEP : 128] = dbuf[d_from + k, 128:NB, 128:NB]
+    blocks.append(outer(5, tails.at[0], tails.at[1], across_chip))
+    blocks[-1].start()
 
     wts[...] = jnp.zeros_like(wts)
     load_v.wait()
@@ -177,9 +191,6 @@
     vectors = outer(4, raw.at[:, edge_out], edges, across_chip)
     vectors.start()
 
-    pl.semaphore_wait(round1, len(links))
-    tell(round2, links + [far[0], far[ZL - 2]])
-
     ICI, CHIP = 0, 1
 
     def on_side(side, j):
@@ -204,8 +215,6 @@
         keep = lanes_nb < size
         wts[i + DEEP - 1, at_row, 0:NB] = jnp.where(keep, value, 0.0).astype(BF16)
 
-    for load in (load_s, load_p, load_c, load_d):
-        load.wait()
     own_size = [sizes[core * NE + i] for i in range(NE)]
     for i in range(NE):
         put_weights(i, 1, dbuf[i + DEEP - 1].astype(F32), own_size[i])
@@ -299,23 +308,49 @@
         for j in range(k + 1 - DEEP, k + 1):
             element(t0 + k, on_side(side, j), j >= 0 or k == DEEP - 2)
 
-    def pass_on(k, side, source, target, skip, n):
+    def pass_on(k, source, target, skip, n):
         v, w = buf.at[source], buf.at[target]
-        left_side = first if side == ICI else jnp.logical_not(first)
-        src = slot(jnp.where(left_side, skip, NE - n - skip), n)
-        dst = slot(jnp.where(left_side, NE + skip, -n - skip), n)
-        return outer(k, v.at[:, src], w.at[:, dst], across_chip if side == ICI else partner)
-
-    second = [pass_on(5 + side, side, 0, 2, DEEP - 2, 1) for side in (ICI, CHIP)]
-    third = [pass_on(7 + side, side, 1, 3, 0, DEEP) for side in (ICI, CHIP)]
+        src = slot(jnp.where(first, NE - n - skip, skip), n)
+        dst = slot(jnp.where(first, -n - skip, NE + skip), n)
+        return outer(k, v.at[:, src], w.at[:, dst], partner)
+
+    second = pass_on(6, 0, 2, DEEP - 2, 1)
+    third = pass_on(7, 1, 3, 0, DEEP)
+    packed_copy = outer(8, packed.at[0], packed.at[1], across_chip)
+    sent = [(1, j) for j in range(DEEP)] + [(0, DEEP - 2)]
+
+    def pack():
+        for k, (source, j) in enumerate(sent):
+            at_slot = on_side(ICI, j)
+            start = aligned(PAD * (at_slot + DEEP), PAD)
+            packed[0, :, 128 * k : 128 * (k + 1)] = buf[source, :, pl.ds(start, 128)]
+            x = buf[source, :, pl.ds(aligned(start + 128, 128), 128)].astype(F32)
+            if k:
+                x = pltpu.roll(x, REST * k, 1)
+            rest = x if k == 0 else rest + x
+        packed[0, :, 512:640] = rest.astype(BF16)
+
+    def unpack():
+        rest = packed[1, :, 512:640].astype(F32)
+        for k, (source, j) in enumerate(sent):
+            start = aligned(PAD * (on_side(ICI, -1 - j) + DEEP), PAD)
+            buf[source + 2, :, pl.ds(start, 128)] = packed[1, :, 128 * k : 128 * (k + 1)]
+            x = pltpu.roll(rest, 128 - REST * k, 1) if k else rest
+            x = jnp.where(lanes_pad[:, 0:128] < REST, x, 0.0).astype(BF16)
+            buf[source + 2, :, pl.ds(aligned(start + 128, 128), 128)] = x
 
     def first_steps(side):
         for k in range(DEEP):
             side_steps(0, side, k)
-            if k == DEEP - 2:
-                second[side].start()
-        third[side].start()
-
+        if side == CHIP:
+            second.start()
+            third.start()
+        else:
+            pack()
+            packed_copy.start()
+
+    pl.semaphore_wait(round1, len(links))
+    tell(round2, links + [far[0], far[ZL - 2]])
     side_weights(CHIP)
     inside(0)
     first_steps(CHIP)
@@ -323,6 +358,14 @@
     tell(round3, links)
     for copy in blocks:
         copy.wait_recv()
+    c_got, d_got = jnp.where(first, 0, DEEP + NE), jnp.where(first, 0, DEEP - 1 + NE)
+    for k in range(DEEP):
+        cbuf[c_got + k, :, 128:NB] = tails[1, :, REST * k : REST * (k + 1)]
+    for k in range(n_e):
+        turned = nt_dot(eye[0:128, 0:128], dbuf[d_got + k, 128:NB, 0:128])
+        dbuf[d_got + k, 0:128, 128:NB] = turned.astype(BF16)
+        corner = tails[1, REST * k : REST * (k + 1), REST * DEEP : 128]
+        dbuf[d_got + k, 128:NB, 128:NB] = corner
     side_weights(ICI)
     vectors.wait_recv()
     for j in range(-1, -DEEP - 1, -1):
@@ -330,11 +373,14 @@
         expand(on_side(ICI, j), number(sizes, sizes_out, ICI, j), edges, column)
     first_steps(ICI)
     inside(DEEP)
-    for side in (CHIP, ICI):
-        second[side].wait_recv()
-        third[side].wait_recv()
-        for k in range(DEEP):
-            side_steps(DEEP, side, k)
+    second.wait_recv()
+    third.wait_recv()
+    for k in range(DEEP):
+        side_steps(DEEP, CHIP, k)
+    packed_copy.wait_recv()
+    unpack()
+    for k in range(DEEP):
+        side_steps(DEEP, ICI, k)
 
     pl.semaphore_wait(round3, len(links))
 
@@ -571,7 +617,7 @@
         def _():
             along.wait_send()
 
-    for copy in sends + blocks + [vectors, swap] + second + third:
+    for copy in sends + blocks + [vectors, swap, second, third, packed_copy]:
         copy.wait_send()
     for write in writes:
         write.wait()
@@ -594,6 +640,8 @@
             pltpu.VMEM((NE + 2 * DEEP, NB, NB), BF16),
             pltpu.VMEM((ROWS, COLS + EDGE), BF16),
             pltpu.VMEM((ROWS, EDGE), BF16),
+            pltpu.VMEM((2, NB, 128), BF16),
+            pltpu.VMEM((2, ROWS, 640), BF16),
             pltpu.VMEM((2, CHIPS, ROWS, COLS), BF16),
             pltpu.VMEM((NY, 2, ROWS, ROWS), F32),
             pltpu.VMEM((NY, 2, HALFROWS, ROWS), BF16),

time: 65.2 us -> 63 us (0.966)
  Pallas kernels: 63.3 us -> 61.1 us
    pallas_call x1, Pallas kernels: 63.3 us -> 61.1 us  [shards(): pl.pallas_call(functools.partial(kernel, total_rows), out_shape=[jax.Shap...]
where the time goes in v6:
time: 63 us; the launch traced here: 62.8 us
  Pallas kernels  61.1 us (97%)
  other arithmetic  1.74 us (3%)
    pallas_call x1, Pallas kernels, shards(): pl.pallas_call(functools.partial(kernel, total_rows), out_shape=[jax.Shap...  61.1 us
    concatenate x1, other arithmetic, shards(): return jnp.concatenate(halves, axis=1)  1.74 us

profile of v6, /device:TPU:1, one launch (start us, length us, event | category | flops | bytes accessed | tf_op | source)
XLA Modules:
  0.0 62.8 jit_solution(15085068582637352157)
XLA Ops:
  0.0 61.1 %filter_step.1 = (bf16[64,1280]{1,0:T(8,128)(2,1)}, bf16[64,1280]{1,0:T(8,128)(2,1)}) custom-call(s32[16]{0:T(128)} %sizes_hbm.1, s32[16]{0:T(128)} %pattern_hbm.1, bf16[16,160,160]{2,1,0:T(8,128)(2,1)} %hd.1, bf16[16,160,160]{2,1,0:T(8,128)(2,1)} %hc.1, bf16[64,2560]{1,0:T(8,128)(2,1)} %bands.1), custom_call_target="tpu_custom_call" | custom-call | tf_op jit(solution)/shard_map/filter_step/pallas_call | solution.py:631
  61.1 1.7 %pad_maximum_fusion = bf16[64,2560]{1,0:T(8,128)(2,1)} fusion(bf16[64,1280]{1,0:T(8,128)(2,1)} %get-tuple-element.8, bf16[64,1280]{1,0:T(8,128)(2,1)} %get-tuple-element.7), kind=kLoop, calls=%fused_computation | loop fusion | flops 655360 | bytes 655360 | tf_op jit(solution)/shard_map/concatenate | solution.py:675

commit v7 on v6

--- a/solution.py
+++ b/solution.py
@@ -66,6 +66,7 @@
     sqs,
     sqr,
     wfull,
+    halfsum,
     obuf,
     sizes,
     pattern,
@@ -277,15 +278,20 @@
         column = jnp.where(first, COLS + NB * (-1 - j), EDGE + NB * j)
         expand(on_side(CHIP, j), number(sizes, sizes_out, CHIP, j), raw, column)
 
+    plan = [
+        (0, None, [1]),
+        (1, 0, [0, 2]),
+        (0, 1, [1, 3]),
+        (3, 2, [2]),
+        (2, 3, [3]),
+        (3, 2, [2]),
+    ]
+
     def element(t, i, own):
-        now, prior, targets = [
-            (0, None, [1]),
-            (1, 0, [0, 2]),
-            (0, 1, [1, 3]),
-            (3, 2, [2]),
-            (2, 3, [3]),
-            (3, 2, [2]),
-        ][t]
+        store(t, i, own, stepped(t, i))
+
+    def stepped(t, i):
+        now, prior, _ = plan[t]
         acc = jnp.dot(
             buf[now, :, slot(i - 1, 3)], wts[i + DEEP - 1], preferred_element_type=F32
         )
@@ -294,8 +300,10 @@
             nxt = shifted * (1.0 / HALF)
         else:
             nxt = shifted * (2.0 / HALF) - buf[prior, :, slot(i)].astype(F32)
-        nxt = nxt.astype(BF16)
-        for target in targets:
+        return nxt.astype(BF16)
+
+    def store(t, i, own, nxt):
+        for target in plan[t][2]:
             if own or target < 2 or t >= DEEP:
                 buf[target, :, slot(i)] = nxt
 
@@ -305,8 +313,10 @@
                 element(t0 + k, i, True)
 
     def side_steps(t0, side, k):
-        for j in range(k + 1 - DEEP, k + 1):
-            element(t0 + k, on_side(side, j), j >= 0 or k == DEEP - 2)
+        level = range(k + 1 - DEEP, k + 1)
+        made = [stepped(t0 + k, on_side(side, j)) for j in level]
+        for j, nxt in zip(level, made):
+            store(t0 + k, on_side(side, j), j >= 0 or k == DEEP - 2, nxt)
 
     def pass_on(k, source, target, skip, n):
         v, w = buf.at[source], buf.at[target]
@@ -425,13 +435,12 @@
     from_x = gather(0, chip, None, xpeer)
     from_dn.append(gather(2, chip, high, yup))
     from_up.append(gather(4, chip, low, ydn))
-    share(0, chip)
 
     r128 = lax.broadcasted_iota(jnp.int32, (ROWS, ROWS), 0)
     c128 = lax.broadcasted_iota(jnp.int32, (ROWS, ROWS), 1)
 
-    def gram(part, g, o):
-        strip[o, part] = nt_dot(held[g], held[side + (y + o) % NY])
+    def gram(which, g, o):
+        strip[o, which] = nt_dot(held[g], held[side + (y + o) % NY])
 
     def squares(k, s, who):
         copy = remote(sqs.at[s], sqr.at[k], sq_send.at[k], sq_recv.at[k], who)
@@ -518,6 +527,7 @@
     gram(1, peer_chip, 2)
     last_sums = over_cores(last)
     to_owners(last, last_sums)
+    share(0, chip)
     share(1, side + y_dn)
     share(2, side + y_up)
     share(3, side + y_far)
@@ -567,18 +577,18 @@
         here = jnp.full((1, ROWS), (zl + NY - y) % NY, jnp.int32) == o
         sq_row = jnp.where(here, by_offset[o], sq_row)
     scale_row = lax.rsqrt(sq_row + EPS)
-    for part in range(2):
-        lanes = lax.rsqrt((sqs[3, 0:1] if part == 0 else sqr[14, 0:1]) + EPS)
+    for rows_of in range(2):
+        lanes = lax.rsqrt((sqs[3, 0:1] if rows_of == 0 else sqr[14, 0:1]) + EPS)
         row_scale = jnp.sum(jnp.where(same, lanes, 0.0), axis=1, keepdims=True)
-        value = total[part]
+        value = total[rows_of]
         ident = jnp.zeros_like(value)
-        if part == 0:
+        if rows_of == 0:
             unit = jnp.logical_and(same, jnp.full(same.shape, zl - y, jnp.int32) == 0)
             value = jnp.where(unit, sq_row, value)
             ident = jnp.where(unit, 1.5, 0.0)
         normed = row_scale * value * scale_row
         w = math.sqrt(total_rows) * scale_row * (ident - 0.5 * normed)
-        s4[part] = w.astype(BF16)
+        s4[rows_of] = w.astype(BF16)
 
     g_cols = pl.ds(pl.multiple_of(g * ROWS, ROWS), ROWS)
     place = wfull.at[pl.ds(pl.multiple_of(xl * quarter, quarter), quarter), g_cols]
@@ -593,17 +603,34 @@
     share(7, far_side + y_far)
     for copy in shared:
         copy.wait_recv()
-    for copy in copies:
+    near_cols = pl.ds(pl.multiple_of(side * ROWS, 128), NY * ROWS)
+    far_cols = pl.ds(pl.multiple_of(far_side * ROWS, 128), NY * ROWS)
+    for copy in copies[: XL * ZL - 1]:
         copy.wait_recv()
     put.wait()
+    for h in range(2):
+        whole = fall.at[h].reshape(BANDS, COLS)
+        for k in range(COLS // PAD):
+            halfsum[h, :, PAD * k : PAD * (k + 1)] = jnp.dot(
+                wfull[:, near_cols],
+                whole[near_cols, PAD * k : PAD * (k + 1)],
+                preferred_element_type=F32,
+            )
+    for copy in copies[XL * ZL - 1 :]:
+        copy.wait_recv()
     sends += copies
 
     writes = []
     for h in range(2):
         whole = fall.at[h].reshape(BANDS, COLS)
         for k in range(COLS // PAD):
-            obuf[h, :, PAD * k : PAD * (k + 1)] = jnp.dot(
-                wfull[...], whole[:, PAD * k : PAD * (k + 1)], preferred_element_type=F32
+            more = jnp.dot(
+                wfull[:, far_cols],
+                whole[far_cols, PAD * k : PAD * (k + 1)],
+                preferred_element_type=F32,
+            )
+            obuf[h, :, PAD * k : PAD * (k + 1)] = (
+                halfsum[h, :, PAD * k : PAD * (k + 1)] + more
             ).astype(BF16)
         write = pltpu.make_async_copy(obuf.at[h], (out_low, out_high)[h], local_sem.at[3 + 4 * h])
         write.start()
@@ -654,6 +681,7 @@
             pltpu.VMEM((4, CHIPS, ROWS), F32),
             pltpu.VMEM((15, CHIPS, ROWS), F32),
             pltpu.VMEM((HALFROWS, BANDS), BF16),
+            pltpu.VMEM((2, HALFROWS, COLS), F32),
             pltpu.VMEM((2, HALFROWS, COLS), BF16),
             *[pltpu.SMEM((2 * NE,), jnp.int32)] * 4,
             *[pltpu.SemaphoreType.REGULAR] * 3,

time: 63 us -> 62.6 us (level)
  no operation moved by 1% of the time
where the time goes in v7:
time: 62.6 us; the launch traced here: 62.5 us
  Pallas kernels  60.7 us (97%)
  other arithmetic  1.74 us (3%)
    pallas_call x1, Pallas kernels, shards(): pl.pallas_call(functools.partial(kernel, total_rows), out_shape=[jax.Shap...  60.7 us
    concatenate x1, other arithmetic, shards(): return jnp.concatenate(halves, axis=1)  1.74 us

profile of v7, /device:TPU:1, one launch (start us, length us, event | category | flops | bytes accessed | tf_op | source)
XLA Modules:
  0.0 62.5 jit_solution(954568221507610055)
XLA Ops:
  0.0 60.7 %filter_step.1 = (bf16[64,1280]{1,0:T(8,128)(2,1)}, bf16[64,1280]{1,0:T(8,128)(2,1)}) custom-call(s32[16]{0:T(128)} %sizes_hbm.1, s32[16]{0:T(128)} %pattern_hbm.1, bf16[16,160,160]{2,1,0:T(8,128)(2,1)} %hd.1, bf16[16,160,160]{2,1,0:T(8,128)(2,1)} %hc.1, bf16[64,2560]{1,0:T(8,128)(2,1)} %bands.1), custom_call_target="tpu_custom_call" | custom-call | tf_op jit(solution)/shard_map/filter_step/pallas_call | solution.py:658
  60.7 1.7 %pad_maximum_fusion = bf16[64,2560]{1,0:T(8,128)(2,1)} fusion(bf16[64,1280]{1,0:T(8,128)(2,1)} %get-tuple-element.8, bf16[64,1280]{1,0:T(8,128)(2,1)} %get-tuple-element.7), kind=kLoop, calls=%fused_computation | loop fusion | flops 655360 | bytes 655360 | tf_op jit(solution)/shard_map/concatenate | solution.py:703

commit v8 on v7

--- a/solution.py
+++ b/solution.py
@@ -44,8 +44,7 @@
     hd,
     hc,
     bands,
-    out_low,
-    out_high,
+    out,
     wts,
     buf,
     dbuf,
@@ -67,7 +66,6 @@
     sqr,
     wfull,
     halfsum,
-    obuf,
     sizes,
     pattern,
     sizes_out,
@@ -620,7 +618,6 @@
         copy.wait_recv()
     sends += copies
 
-    writes = []
     for h in range(2):
         whole = fall.at[h].reshape(BANDS, COLS)
         for k in range(COLS // PAD):
@@ -629,12 +626,9 @@
                 whole[far_cols, PAD * k : PAD * (k + 1)],
                 preferred_element_type=F32,
             )
-            obuf[h, :, PAD * k : PAD * (k + 1)] = (
+            out[:, COLS * h + PAD * k : COLS * h + PAD * (k + 1)] = (
                 halfsum[h, :, PAD * k : PAD * (k + 1)] + more
             ).astype(BF16)
-        write = pltpu.make_async_copy(obuf.at[h], (out_low, out_high)[h], local_sem.at[3 + 4 * h])
-        write.start()
-        writes.append(write)
     for o in range(NY):
         crossing, _ = to_owner(o, 1)
         crossing.wait_send()
@@ -646,8 +640,6 @@
 
     for copy in sends + blocks + [vectors, swap, second, third, packed_copy]:
         copy.wait_send()
-    for write in writes:
-        write.wait()
 
 
 def shards(basis_sizes, coupling_pattern, h_diag, h_couple, bands):
@@ -655,11 +647,11 @@
     hbm = pl.BlockSpec(memory_space=pltpu.HBM)
     dma = pltpu.SemaphoreType.DMA
     quarter = HALFROWS // XL
-    halves = pl.pallas_call(
+    return pl.pallas_call(
         functools.partial(kernel, total_rows),
-        out_shape=[jax.ShapeDtypeStruct((HALFROWS, COLS), BF16)] * 2,
+        out_shape=pltpu.VMEM(bands.shape, BF16),
         in_specs=[hbm] * 5,
-        out_specs=[hbm, hbm],
+        out_specs=pl.BlockSpec(memory_space=pltpu.VMEM),
         scratch_shapes=[
             pltpu.VMEM((NE + 2 * DEEP - 2, 3 * PAD, PAD), BF16),
             pltpu.VMEM((4, ROWS, PAD * (NE + 2 * DEEP)), BF16),
@@ -682,7 +674,6 @@
             pltpu.VMEM((15, CHIPS, ROWS), F32),
             pltpu.VMEM((HALFROWS, BANDS), BF16),
             pltpu.VMEM((2, HALFROWS, COLS), F32),
-            pltpu.VMEM((2, HALFROWS, COLS), BF16),
             *[pltpu.SMEM((2 * NE,), jnp.int32)] * 4,
             *[pltpu.SemaphoreType.REGULAR] * 3,
             dma((8,)),
@@ -696,11 +687,10 @@
             dma((15,)),
         ],
         compiler_params=pltpu.CompilerParams(
-            collective_id=0, has_side_effects=True, vmem_limit_bytes=67043328
+            collective_id=0, has_side_effects=True, vmem_limit_bytes=62000000
         ),
         name="filter_step",
     )(basis_sizes, coupling_pattern, h_diag, h_couple, bands)
-    return jnp.concatenate(halves, axis=1)
 
 
 def solution(mesh):

time: 62.6 us -> 61 us (0.974)
  other arithmetic: 1.74 us -> 0 us
  local copies, waits for them, and re-layouts: 0 us -> 0.73 us
    concatenate x1 -> x0, other arithmetic: 1.74 us -> none  [shards(): return jnp.concatenate(halves, axis=1)]
    unnamed x0 -> x1, local copies, waits for them, and re-layouts: none -> 0.73 us
where the time goes in v8:
time: 61 us; the launch traced here: 60.9 us
  Pallas kernels  60.2 us (99%)
  local copies, waits for them, and re-layouts  0.73 us (1%)
    pallas_call x1, Pallas kernels, shards(): pl.pallas_call(functools.partial(kernel, total_rows), out_shape=pltpu.VME...  60.2 us

profile of v8, /device:TPU:1, one launch (start us, length us, event | category | flops | bytes accessed | tf_op | source)
XLA Modules:
  0.0 60.9 jit_solution(13821617449057803512)
XLA Ops:
  0.0 60.2 %filter_step.1 = bf16[64,2560]{1,0:T(8,128)(2,1)S(1)} custom-call(s32[16]{0:T(128)} %sizes_hbm.1, s32[16]{0:T(128)} %pattern_hbm.1, bf16[16,160,160]{2,1,0:T(8,128)(2,1)} %hd.1, bf16[16,160,160]{2,1,0:T(8,128)(2,1)} %hc.1, bf16[64,2560]{1,0:T(8,128)(2,1)} %bands.1), custom_call_target="tpu_custom_call" | custom-call | tf_op jit(solution)/shard_map/filter_step/pallas_call | solution.py:650
  60.2 0.7 %copy.7 = bf16[64,2560]{1,0:T(8,128)(2,1)} copy(bf16[64,2560]{1,0:T(8,128)(2,1)S(1)} %filter_step.1) | data formatting | bytes 655360

commit v9 on v8

--- a/solution.py
+++ b/solution.py
@@ -469,7 +469,7 @@
         rows = pl.ds(pl.multiple_of(xl_ * quarter, quarter), quarter)
         who = at(xl_ * ZN + zh * ZL + col, b)
         copy = remote(
-            s2.at[o, :, rows], r2.at[j - 1], red_send.at[j + 4], red_recv.at[j + 4], who
+            s2.at[o, :, rows], r2.at[j], red_send.at[j + 4], red_recv.at[j + 4], who
         )
         return copy, col != zl
 
@@ -531,12 +531,12 @@
     share(3, side + y_far)
     share(4, peer_chip)
 
-    copies = [stage(4 + j, r2.at[j - 1], r2.at[j - 1], near[j - 1]) for j in range(1, XL * ZL)]
+    copies = [stage(4 + j, r2.at[j], r2.at[j], near[j - 1]) for j in range(1, XL * ZL)]
     for copy in copies:
         copy.wait_recv()
     total = strip[(zl + NY - y) % NY, :, piece_rows, :]
     for j in range(1, XL * ZL):
-        total = total + r2[j - 1].astype(F32)
+        total = total + r2[j].astype(F32)
     s3[...] = total.astype(BF16)
     copies = [stage(11 + j, s3, r3.at[j - 1], far[j - 1]) for j in range(1, ZL)]
     for copy in copies:
@@ -666,7 +666,7 @@
             pltpu.VMEM((NY, 2, HALFROWS, ROWS), BF16),
             pltpu.VMEM((NY, 2, HALFROWS, ROWS), BF16),
             pltpu.VMEM((NY, 2, HALFROWS, ROWS), BF16),
-            pltpu.VMEM((XL * ZL - 1, 2, quarter, ROWS), BF16),
+            pltpu.VMEM((XL * ZL, 2, quarter, ROWS), BF16),
             pltpu.VMEM((2, quarter, ROWS), BF16),
             pltpu.VMEM((ZL - 1, 2, quarter, ROWS), BF16),
             pltpu.VMEM((2, quarter, ROWS), BF16),

time: 61 us -> 61 us (level)
  no operation moved by 1% of the time
where the time goes in v9:
time: 61 us; the launch traced here: 60.9 us
  Pallas kernels  60.2 us (99%)
  local copies, waits for them, and re-layouts  0.73 us (1%)
    pallas_call x1, Pallas kernels, shards(): pl.pallas_call(functools.partial(kernel, total_rows), out_shape=pltpu.VME...  60.2 us

profile of v9, /device:TPU:1, one launch (start us, length us, event | category | flops | bytes accessed | tf_op | source)
XLA Modules:
  0.0 60.9 jit_solution(3189311513888923209)
XLA Ops:
  0.0 60.2 %filter_step.1 = bf16[64,2560]{1,0:T(8,128)(2,1)S(1)} custom-call(s32[16]{0:T(128)} %sizes_hbm.1, s32[16]{0:T(128)} %pattern_hbm.1, bf16[16,160,160]{2,1,0:T(8,128)(2,1)} %hd.1, bf16[16,160,160]{2,1,0:T(8,128)(2,1)} %hc.1, bf16[64,2560]{1,0:T(8,128)(2,1)} %bands.1), custom_call_target="tpu_custom_call" | custom-call | tf_op jit(solution)/shard_map/filter_step/pallas_call | solution.py:650
  60.2 0.7 %copy.7 = bf16[64,2560]{1,0:T(8,128)(2,1)} copy(bf16[64,2560]{1,0:T(8,128)(2,1)S(1)} %filter_step.1) | data formatting | bytes 655360

commit v10 on v9

--- a/solution.py
+++ b/solution.py
@@ -392,22 +392,23 @@
 
     pl.semaphore_wait(round3, len(links))
 
-    final = 2
-    chunks = {}
-    for i in range(NE):
-        start = (NB * i) // 128
-        off = NB * i - 128 * start
-        x = buf[final, :, slot(i)].astype(F32)
-        if off:
-            x = pltpu.roll(x, off, 1)
-        for k in range(2):
-            part = x[:, 128 * k : 128 * (k + 1)]
-            at_chunk = start + k
-            chunks[at_chunk] = chunks[at_chunk] + part if at_chunk in chunks else part
-        done_to = COLS // 128 if i == NE - 1 else (NB * (i + 1)) // 128
-        for c in sorted(chunks):
-            if c < done_to:
-                fall[core, chip, :, 128 * c : 128 * (c + 1)] = chunks.pop(c).astype(BF16)
+    def compact(rows):
+        final = 2
+        chunks = {}
+        for i in range(NE):
+            start = (NB * i) // 128
+            off = NB * i - 128 * start
+            x = buf[final, rows, slot(i)].astype(F32)
+            if off:
+                x = pltpu.roll(x, off, 1)
+            for k in range(2):
+                part = x[:, 128 * k : 128 * (k + 1)]
+                at_chunk = start + k
+                chunks[at_chunk] = chunks[at_chunk] + part if at_chunk in chunks else part
+            done_to = COLS // 128 if i == NE - 1 else (NB * (i + 1)) // 128
+            for c in sorted(chunks):
+                if c < done_to:
+                    fall[core, chip, rows, 128 * c : 128 * (c + 1)] = chunks.pop(c).astype(BF16)
 
     y_up, y_dn, y_far = (y + 1) % NY, (y + NY - 1) % NY, (y + 2) % NY
     peer_chip = (1 - xh) * NY + y
@@ -428,7 +429,9 @@
         shared.append(copy)
 
     sends, shared = [], []
+    compact(low)
     from_dn = [gather(1, chip, low, yup)]
+    compact(high)
     from_up = [gather(3, chip, high, ydn)]
     from_x = gather(0, chip, None, xpeer)
     from_dn.append(gather(2, chip, high, yup))

time: 61 us -> 61 us (level)
  no operation moved by 1% of the time
where the time goes in v10:
time: 61 us; the launch traced here: 60.9 us
  Pallas kernels  60.1 us (99%)
  local copies, waits for them, and re-layouts  0.73 us (1%)
    pallas_call x1, Pallas kernels, shards(): pl.pallas_call(functools.partial(kernel, total_rows), out_shape=pltpu.VME...  60.1 us

profile of v10, /device:TPU:1, one launch (start us, length us, event | category | flops | bytes accessed | tf_op | source)
XLA Modules:
  0.0 60.9 jit_solution(10451267255455973516)
XLA Ops:
  0.0 60.1 %filter_step.1 = bf16[64,2560]{1,0:T(8,128)(2,1)S(1)} custom-call(s32[16]{0:T(128)} %sizes_hbm.1, s32[16]{0:T(128)} %pattern_hbm.1, bf16[16,160,160]{2,1,0:T(8,128)(2,1)} %hd.1, bf16[16,160,160]{2,1,0:T(8,128)(2,1)} %hc.1, bf16[64,2560]{1,0:T(8,128)(2,1)} %bands.1), custom_call_target="tpu_custom_call" | custom-call | tf_op jit(solution)/shard_map/filter_step/pallas_call | solution.py:653
  60.1 0.7 %copy.7 = bf16[64,2560]{1,0:T(8,128)(2,1)} copy(bf16[64,2560]{1,0:T(8,128)(2,1)S(1)} %filter_step.1) | data formatting | bytes 655360
